TPU v7x, 32 devices: a whole 2x2x4 slice. The times are simulated.
32 devices in a mesh: lat: 8 (over z, y), lon: 4 (over x, core).
Axes of the slice: x: 2, y: 2, z: 4, core: 2. Of those that a mesh axis runs over, the one named last changes fastest.
Arguments:
- grid_fields: bfloat16 [1280, 50, 3, 2560], P('lat', None, None, 'lon'), may hold values from -6 to 6
- legendre: bfloat16 [512, 1280, 640], P(('lat', 'lon')), may hold values from -0.15625 to 0.15625
- wave_of_slot: int32 [512], replicated, may hold values from 0 to 511, as said below
- energy_weight: float32 [3, 640], replicated, may hold values from 0.1 to 10
Outputs:
- spectral: bfloat16 [50, 3, 512, 2, 640], P(None, None, ('lat', 'lon'))
- gram_matrix: float32 [50, 50], replicated
Inputs may be any that keep to these rules, and one draw needn't show every extreme that they name: `wave_of_slot`: every wavenumber 0 to 511 stands in exactly one slot; slot d * 16 + r holds a wavenumber of r * 32 to r * 32 + 31.
All inputs are finite; a program needn't handle non-finite values.
Results may differ from a plain program's by a relative error of at most 0.0043.
Values may be sent and summed in bfloat16 or wider, within the bound.
No kernel may reach another device: no remote copies, remote signals or barrier semaphores. Data moves between devices by JAX's collectives and lax.ppermute only.
A program may use at most 256 MiB of HBM per device.

v0:
```python
import math

import jax
import jax.numpy as jnp
from jax import lax
from jax.sharding import PartitionSpec as P

M = 512
NT = 640
LEV = 3


def make_trig(wave_list, lon_total):
    longitude = jnp.arange(lon_total, dtype=jnp.int32)
    phase_index = longitude[:, None] * wave_list[None, :] % lon_total
    angles = phase_index.astype(jnp.float32) * (2.0 * math.pi / lon_total)
    stacked = jnp.stack([jnp.cos(angles), -jnp.sin(angles)], axis=2)
    return stacked.reshape(lon_total, 2 * wave_list.shape[0]).astype(jnp.bfloat16)


def on_device(grid_fields, legendre, wave_of_slot, energy_weight):
    lat_dev, vectors, levels, lon_dev = grid_fields.shape
    bands = lax.axis_size("lat")
    sectors = lax.axis_size("lon")
    lon_total = lon_dev * sectors
    per_dev = legendre.shape[0]
    degrees = legendre.shape[2]
    fields = vectors * levels
    band_rows = lat_dev // sectors
    norm_scale = 1.0 / math.sqrt(lon_total)
    trig_table = make_trig(wave_of_slot, lon_total)
    moved_rows = lax.all_to_all(grid_fields, "lon", split_axis=0, concat_axis=3, tiled=True)
    product = jnp.dot(
        moved_rows.reshape(-1, lon_total), trig_table, preferred_element_type=jnp.float32
    )
    fourier = product.reshape(band_rows, fields, -1) * norm_scale
    gathered = lax.all_to_all(
        lax.all_to_all(fourier, "lat", split_axis=2, concat_axis=0, tiled=True),
        "lon",
        split_axis=2,
        concat_axis=0,
        tiled=True,
    )
    cols_here = gathered.shape[2]
    columns = gathered.reshape(sectors, bands, band_rows, fields, cols_here).transpose(
        1, 0, 2, 3, 4
    )
    columns = columns.reshape(bands * lat_dev, fields, cols_here)
    columns = columns.reshape(bands * lat_dev, fields, per_dev, 2)
    device_slot = (lax.axis_index("lat") * sectors + lax.axis_index("lon")) * per_dev
    own_waves = lax.dynamic_slice_in_dim(wave_of_slot, device_slot, per_dev, 0)
    degree_index = jnp.arange(degrees, dtype=jnp.int32)
    tri_mask = (degree_index[None, :] >= own_waves[:, None]).astype(jnp.float32)
    legendre_table = legendre.astype(jnp.float32) * tri_mask[:, None, :]
    spectral = jnp.einsum(
        "aftp,tan->ftpn", columns, legendre_table, precision=lax.Precision.HIGHEST
    )
    spectral = spectral.reshape(vectors, levels, per_dev, 2, degrees)
    factor = jnp.where(own_waves == 0, 1.0, 2.0).astype(jnp.float32)
    weighted = spectral * factor[None, None, :, None, None] * energy_weight[None, :, None, None, :]
    partial_value = jnp.dot(
        spectral.reshape(vectors, -1),
        weighted.reshape(vectors, -1).T,
        precision=lax.Precision.HIGHEST,
    )
    gram_matrix = lax.psum(partial_value, ("lat", "lon")) / (LEV * M * NT)
    return (spectral.astype(jnp.bfloat16), gram_matrix)


def solution(mesh):
    placed = (P("lat", None, None, "lon"), P(("lat", "lon"), None, None), P(), P())
    return jax.shard_map(
        on_device,
        mesh=mesh,
        in_specs=placed,
        out_specs=(P(None, None, ("lat", "lon"), None, None), P()),
        check_vma=False,
    )
```

profile of v0, /device:TPU:0, one launch (start us, length us, event | category | flops | bytes accessed | tf_op | source)
XLA Modules:
  0.0 2192.7 jit_solution(3052948345299898282)
XLA Ops:
  0.6 22.1 %copy.47 = bf16[160,50,3,640]{3,1,2,0:T(8,128)(2,1)} copy(bf16[160,50,3,640]{3,0,2,1:T(8,128)(2,1)} %param.4) | data formatting | bytes 61440000 | tf_op args[0]
  32.8 22.3 %cosine_convert_fusion = (bf16[2560,512,1]{1,0,2:T(8,128)(2,1)S(1)}, bf16[2560,512,1]{1,0,2:T(8,128)(2,1)S(1)}) fusion(s32[512]{0:T(512)S(1)} %copy-done.1), kind=kLoop, calls=%fused_computation.14 | loop fusion | flops 15728640 | bytes 5244928 | tf_op jit(solution)/shard_map/convert
  57.9 13.9 copy.46
  71.8 11.6 convert_element_type.43
  83.4 321.9 %all-to-all-done = bf16[160,50,3,640]{3,1,2,0:T(8,128)(2,1)} async-done(((bf16[160,50,3,640]{3,1,2,0:T(8,128)(2,1)}), bf16[160,50,3,640]{3,1,2,0:T(8,128)(2,1)}, u32[]{:S(2)}, u32[]{:S(2)}) %all-to-all-start) | async-done | bytes 30720032 | tf_op jit(solution)/shard_map/all_to_all | solution.py:32
  405.4 27.3 %copy.48 = bf16[4,40,50,3,640]{4,0,3,2,1:T(4,128)(2,1)} copy(bf16[4,40,50,3,640]{4,2,3,1,0:T(8,128)(2,1)} %bitcast.2) | data formatting | bytes 61440000 | tf_op jit(solution)/shard_map/all_to_all | solution.py:32
  432.6 21.6 copy.67
  454.2 39.4 %multiply_bitcast_fusion = f32[6000,1024]{1,0:T(8,128)} fusion(bf16[2560,1024]{0,1:T(8,128)(2,1)} %convert_element_type.43, bf16[6000,2560]{1,0:T(8,128)(2,1)} %bitcast.48), kind=kOutput, calls=%fused_computation.5 | convolution fusion | flops 31463424000 | bytes 60538880 | tf_op jit(solution)/shard_map/dot_general | solution.py:33
  493.6 19.6 mul.105
  513.3 43.6 %copy.49 = f32[40,150,1024]{1,0,2:T(8,128)} copy(f32[40,150,1024]{2,1,0:T(8,128)} %mul.105) | data formatting | bytes 49152000 | tf_op jit(solution)/shard_map/mul | solution.py:36
  556.9 915.7 %all_to_all.48 = f32[40,150,1024]{1,0,2:T(8,128)} all-to-all(f32[40,150,1024]{1,0,2:T(8,128)} %copy.49), channel_id=1, replica_groups=mesh['lat'=8,'lon'=4] {'lat'}, dimensions={2} | all-to-all | bytes 49152000 | tf_op jit(solution)/shard_map/all_to_all | solution.py:38
  1472.6 36.6 %copy.51 = f32[8,40,150,128]{3,1,0,2:T(8,128)} copy(f32[8,40,150,128]{2,1,3,0:T(8,128)} %bitcast.44) | data formatting | bytes 49152000 | tf_op jit(solution)/shard_map/all_to_all | solution.py:38
  1509.2 28.0 %copy.52 = f32[320,150,128]{0,1,2:T(8,128)} copy(f32[320,150,128]{2,0,1:T(8,128)} %bitcast.47) | data formatting | bytes 49152000 | tf_op jit(solution)/shard_map/all_to_all | solution.py:38
  1548.0 322.3 %all-to-all-done.2 = f32[320,150,128]{0,1,2:T(8,128)} async-done(((f32[320,150,128]{0,1,2:T(8,128)}), f32[320,150,128]{0,1,2:T(8,128)}, u32[]{:S(2)}, u32[]{:S(2)}) %all-to-all-start.2) | async-done | bytes 24576032 | tf_op jit(solution)/shard_map/all_to_all | solution.py:37
  1870.3 46.2 %copy.54 = f32[4,320,150,32]{2,3,1,0:T(8,128)} copy(f32[4,320,150,32]{1,2,3,0:T(8,128)} %bitcast.11) | data formatting | bytes 49152000 | tf_op jit(solution)/shard_map/all_to_all | solution.py:37
  1916.5 39.3 %copy.55 = f32[8,4,40,150,32]{3,2,1,0,4:T(8,128)} copy(f32[8,4,40,150,32]{3,4,2,0,1:T(8,128)} %bitcast.45) | data formatting | bytes 49152000 | tf_op jit(solution)/shard_map/transpose | solution.py:45
  1955.7 76.5 %fusion = f32[16,640,150,2]{1,2,3,0:T(8,128)} fusion(f32[1280,150,16,2]{1,0,3,2:T(8,128)} %bitcast.43, bf16[16,1280,640]{2,1,0:T(8,128)(2,1)} %param.5, f32[16,640]{1,0:T(8,128)S(1)} %fusion.11), kind=kOutput, calls=%fused_computation | convolution fusion | flops 47212134400 | bytes 63119360 | tf_op jit(solution)/shard_map/aftp,tan->ftpn/dot_general | solution.py:55
  2051.6 22.5 %copy.58 = f32[150,16,2,640]{3,2,1,0:T(2,128)} copy(f32[150,16,2,640]{3,0,2,1:T(8,128)} %bitcast.42) | data formatting | bytes 24576000 | tf_op jit(solution)/shard_map/aftp,tan->ftpn/transpose | solution.py:55
  2074.1 15.4 reshape_reshape.7
  2089.5 13.2 fusion.5
  2102.6 18.4 copy.59
  2121.0 15.1 mul.112
  2136.1 16.4 fusion.12
  2152.5 39.1 %psum.7 = f32[50,50]{1,0:T(8,128)S(1)} all-reduce(f32[50,50]{1,0:T(8,128)S(1)} %fusion.12), channel_id=1, replica_groups=mesh['lat'=8,'lon'=4] {'lat','lon'}, use_global_device_ids=true, to_apply=%region_0.1 | all-reduce | flops 2500 | bytes 20000 | tf_op jit(solution)/shard_map/psum | solution.py:66
  (14 shorter events, 43.5 us)
Async XLA Ops:
  22.7 10.0 copy-start.1
  22.7 382.6 %all-to-all-start = ((bf16[160,50,3,640]{3,1,2,0:T(8,128)(2,1)}), bf16[160,50,3,640]{3,1,2,0:T(8,128)(2,1)}, u32[]{:S(2)}, u32[]{:S(2)}) async-start(bf16[160,50,3,640]{3,1,2,0:T(8,128)(2,1)} %copy.47), calls=%async_computation | async-start | bytes 68812800 | tf_op jit(solution)/shard_map/all_to_all | solution.py:32
  1537.2 9.7 copy-start
  1537.2 333.1 %all-to-all-start.2 = ((f32[320,150,128]{0,1,2:T(8,128)}), f32[320,150,128]{0,1,2:T(8,128)}, u32[]{:S(2)}, u32[]{:S(2)}) async-start(f32[320,150,128]{0,1,2:T(8,128)} %copy.52), calls=%async_computation.2 | async-start | bytes 59768832 | tf_op jit(solution)/shard_map/all_to_all | solution.py:37
where the time goes:
time: 2210 us; the launch traced here: 2190 us
  blocking collectives  955 us (43%)
  waiting for transfers between devices  644 us (29%)
  local copies, waits for them, and re-layouts  401 us (18%)
  matrix products  132 us (6%)
  other arithmetic  39.7 us (2%)
    all_to_all x1, blocking collectives, on_device(): lax.all_to_all(fourier, 'lat', split_axis=2, concat_axis=0, tiled=True)  916 us
    all_to_all x1, waiting for transfers between devices, on_device(): lax.all_to_all(lax.all_to_all(fourier, 'lat', split_axis=2, concat_axis=0...  322 us
    all_to_all x1, waiting for transfers between devices, on_device(): lax.all_to_all(grid_fields, 'lon', split_axis=0, concat_axis=3, tiled=True)  322 us
    dot_general x1, matrix products, on_device(): jnp.einsum('aftp,tan->ftpn', columns, legendre_table, precision=lax.Preci...  76.5 us
    all_to_all x2, local copies, waits for them, and re-layouts, on_device(): lax.all_to_all(fourier, 'lat', split_axis=2, concat_axis=0, tiled=True)  64.6 us
    mul x2, local copies, waits for them, and re-layouts, on_device(): fourier = product.reshape(band_rows, fields, -1) * norm_scale  63.2 us
    unnamed x7, local copies, waits for them, and re-layouts  55 us
    all_to_all x1, local copies, waits for them, and re-layouts, on_device(): lax.all_to_all(lax.all_to_all(fourier, 'lat', split_axis=2, concat_axis=0...  46.2 us
  transfers between devices with their start and end apart: 2, of which 2 were waited for; matrix products, arithmetic and copies ran while one was open for 2% of the time, Pallas kernels for 0%

commit v1 on v0

v1 whole, which is shorter than its diff:
```python
import functools
import math

import jax
import jax.numpy as jnp
from jax import lax
from jax.experimental import pallas as pl
from jax.experimental.pallas import tpu as pltpu
from jax.sharding import Mesh
from jax.sharding import PartitionSpec as P


CORES = 2
LANES = 128
SUB = 8


def make_trig(wave_list, lon_total):
    longitude = jnp.arange(lon_total, dtype=jnp.int32)
    phase_index = longitude[:, None] * wave_list[None, :] % lon_total
    angles = phase_index.astype(jnp.float32) * (2.0 * math.pi / lon_total)
    stacked = jnp.stack([jnp.cos(angles), -jnp.sin(angles)], axis=2)
    return stacked.reshape(lon_total, 2 * wave_list.shape[0]).astype(jnp.bfloat16)


def plain(grid_fields, legendre, wave_of_slot, energy_weight):
    lat_dev, vectors, levels, lon_dev = grid_fields.shape
    bands = lax.axis_size("lat")
    sectors = lax.axis_size("x") * lax.axis_size("core")
    lon_total = lon_dev * sectors
    per_dev = legendre.shape[0]
    degrees = legendre.shape[2]
    fields = vectors * levels
    band_rows = lat_dev // sectors
    norm_scale = 1.0 / math.sqrt(lon_total)
    lon = ("x", "core")
    trig_table = make_trig(wave_of_slot, lon_total)
    moved_rows = lax.all_to_all(grid_fields, lon, split_axis=0, concat_axis=3, tiled=True)
    product = jnp.dot(
        moved_rows.reshape(-1, lon_total), trig_table, preferred_element_type=jnp.float32
    )
    fourier = product.reshape(band_rows, fields, -1) * norm_scale
    gathered = lax.all_to_all(
        lax.all_to_all(fourier, "lat", split_axis=2, concat_axis=0, tiled=True),
        lon,
        split_axis=2,
        concat_axis=0,
        tiled=True,
    )
    cols_here = gathered.shape[2]
    columns = gathered.reshape(sectors, bands, band_rows, fields, cols_here).transpose(
        1, 0, 2, 3, 4
    )
    columns = columns.reshape(bands * lat_dev, fields, per_dev, 2)
    device_slot = lax.axis_index(("lat", "x", "core")) * per_dev
    own_waves = lax.dynamic_slice_in_dim(wave_of_slot, device_slot, per_dev, 0)
    degree_index = jnp.arange(degrees, dtype=jnp.int32)
    tri_mask = (degree_index[None, :] >= own_waves[:, None]).astype(jnp.float32)
    legendre_table = legendre.astype(jnp.float32) * tri_mask[:, None, :]
    spectral = jnp.einsum(
        "aftp,tan->ftpn", columns, legendre_table, precision=lax.Precision.HIGHEST
    )
    spectral = spectral.reshape(vectors, levels, per_dev, 2, degrees)
    factor = jnp.where(own_waves == 0, 1.0, 2.0).astype(jnp.float32)
    weighted = spectral * factor[None, None, :, None, None] * energy_weight[None, :, None, None, :]
    partial_value = jnp.dot(
        spectral.reshape(vectors, -1),
        weighted.reshape(vectors, -1).T,
        precision=lax.Precision.HIGHEST,
    )
    slots = wave_of_slot.shape[0]
    gram_matrix = lax.psum(partial_value, ("lat", "x", "core")) / (levels * slots * degrees)
    return (spectral.astype(jnp.bfloat16), gram_matrix)


class Rows:
    def __init__(self, fields, lat_dev):
        self.fields = fields
        self.rest = lat_dev % LANES
        self.pack = LANES // self.rest
        self.block = self.pack if fields % self.pack == 0 else fields
        self.blocks = fields // self.block
        self.quads_in = -(-self.block // self.pack)
        self.quads = self.blocks * self.quads_in
        self.width = (self.block + self.quads_in) * LANES
        self.total = self.blocks * self.width

    def full(self, f):
        return f // self.block * self.width + f % self.block * LANES

    def tail(self, q):
        return q // self.quads_in * self.width + (self.block + q % self.quads_in) * LANES

    def quad_of(self, f):
        inner = f % self.block
        return f // self.block * self.quads_in + inner // self.pack, inner % self.pack


def fourier_kernel(scale, rows, with_add, *refs):
    if with_add:
        t0, t1, g0, g1, add, out = refs
    else:
        t0, t1, g0, g1, out = refs

    def packed(g):
        parts = [g[f, :LANES, :] for f in range(rows.block)]
        parts += [g[f, LANES:, :] for f in range(rows.block)]
        spare = rows.width - rows.block * g.shape[1]
        if spare:
            parts.append(jnp.zeros((spare, g.shape[2]), g.dtype))
        return jnp.concatenate(parts, axis=0)

    dims = (((1,), (1,)), ((), ()))
    total = lax.dot_general(t0[...], packed(g0), dims, preferred_element_type=jnp.float32)
    total += lax.dot_general(t1[...], packed(g1), dims, preferred_element_type=jnp.float32)
    total *= scale
    if with_add:
        total += add[...].astype(jnp.float32)
    out[...] = total.astype(out.dtype)


def fourier(t0, t1, g0, g1, scale, rows, add=None):
    cols, lon = t0.shape
    lat_dev = g0.shape[1]
    table = pl.BlockSpec((cols, lon), lambda i: (0, 0))
    field = pl.BlockSpec((rows.block, lat_dev, lon), lambda i: (i, 0, 0))
    wide = pl.BlockSpec((cols, rows.width), lambda i: (0, i))
    args = [t0, t1, g0, g1] + ([] if add is None else [add])
    return pl.pallas_call(
        functools.partial(fourier_kernel, scale, rows, add is not None),
        grid=(rows.blocks,),
        in_specs=[table, table, field, field] + ([] if add is None else [wide]),
        out_specs=wide,
        out_shape=jax.ShapeDtypeStruct((cols, rows.total), jnp.bfloat16),
        compiler_params=pltpu.CompilerParams(vmem_limit_bytes=48 * 2**20),
        cost_estimate=pl.CostEstimate(
            flops=4 * cols * rows.total * lon,
            bytes_accessed=4 * rows.total * lon + 4 * cols * rows.total + 4 * cols * lon,
            transcendentals=0,
        ),
        name="fourier",
    )(*args)


def legendre_kernel(bands, rows, lat_dev, degrees, cof, leg, wave, out):
    fields, pack, rest = rows.fields, rows.pack, rows.rest
    lane = lax.broadcasted_iota(jnp.int32, (CORES * rows.quads * SUB, LANES), 1) // rest

    def stacked(z, starts):
        parts = [
            cof[z * CORES + c, :, at : at + LANES].astype(jnp.float32)
            for c in range(CORES)
            for at in starts
        ]
        return jnp.concatenate(parts, axis=0)

    left = [stacked(z, [rows.full(f) for f in range(fields)]) for z in range(bands)]
    for g in range(bands // pack):
        shards = [None] * pack
        for slot in range(pack):
            tail = stacked(g * pack + slot, [rows.tail(q) for q in range(rows.quads)])
            for j in range(pack):
                shift = (slot - j) % pack * rest
                moved = tail if shift == 0 else pltpu.roll(tail, shift, 1)
                shards[j] = moved if slot == 0 else jnp.where(lane == slot, moved, shards[j])
        pieces = []
        for c in range(CORES):
            for f in range(fields):
                quad, j = rows.quad_of(f)
                at = (c * rows.quads + quad) * SUB
                pieces.append(shards[j][at : at + SUB])
        left.append(jnp.concatenate(pieces, axis=0))
    count = CORES * fields * SUB
    left = jnp.concatenate(left, axis=1)
    slot_of_row = lax.broadcasted_iota(jnp.int32, (count, 1), 0) % SUB // 2
    total = jnp.zeros((count, degrees), jnp.float32)
    for s in range(SUB // 2):
        here = jnp.where(slot_of_row == s, left, 0.0).astype(jnp.bfloat16)
        table = jnp.concatenate(
            [leg[s, z * lat_dev : z * lat_dev + LANES, :] for z in range(bands)]
            + [leg[s, z * lat_dev + LANES : (z + 1) * lat_dev, :] for z in range(bands)],
            axis=0,
        )
        total += jnp.dot(here, table, preferred_element_type=jnp.float32)
    total = total.reshape(CORES * fields, SUB, degrees)
    degree = lax.broadcasted_iota(jnp.int32, (SUB, degrees), 1)
    keep = degree >= wave[:, :1]
    total = jnp.where(keep[None], total, 0.0)
    out[...] = total.astype(out.dtype)


def legendre_sums(cof, leg, waves, rows):
    sources, slot_rows, _ = cof.shape
    fields = rows.fields
    slots, lats, degrees = leg.shape
    bands = sources // CORES
    lat_dev = lats // bands
    return pl.pallas_call(
        functools.partial(legendre_kernel, bands, rows, lat_dev, degrees),
        grid=(slot_rows // SUB,),
        in_specs=[
            pl.BlockSpec((sources, SUB, rows.total), lambda i: (0, i, 0)),
            pl.BlockSpec((SUB // 2, lats, degrees), lambda i: (i, 0, 0)),
            pl.BlockSpec((SUB, LANES), lambda i: (i, 0)),
        ],
        out_specs=pl.BlockSpec((CORES * fields, SUB, degrees), lambda i: (0, i, 0)),
        out_shape=jax.ShapeDtypeStruct((CORES * fields, slot_rows, degrees), jnp.bfloat16),
        compiler_params=pltpu.CompilerParams(vmem_limit_bytes=56 * 2**20),
        cost_estimate=pl.CostEstimate(
            flops=4 * CORES * fields * slot_rows * lats * degrees,
            bytes_accessed=2 * sources * slot_rows * rows.total + 2 * slots * lats * degrees,
            transcendentals=0,
        ),
        name="legendre",
    )(cof, leg, waves)


def gram_kernel(groups, *refs):
    specs = refs[:groups]
    weight, wave, place, out, total = refs[groups:]
    step = pl.program_id(0) * pl.num_programs(1) + pl.program_id(1)
    values = jnp.concatenate([r[...].reshape(-1, r.shape[-1]) for r in specs], axis=0)
    rows, degrees = values.shape
    vectors = rows // SUB
    factor = jnp.where(wave[:, :1] == 0, 1.0, 2.0).astype(jnp.float32)
    scaled = values.astype(jnp.float32).reshape(vectors, SUB, degrees) * (factor * weight[0])[None]
    scaled = scaled.reshape(rows, degrees).astype(jnp.bfloat16)
    part = lax.dot_general(
        scaled, values, (((1,), (1,)), ((), ())), preferred_element_type=jnp.float32
    )

    @pl.when(step == 0)
    def _():
        total[...] = part

    @pl.when(step > 0)
    def _():
        total[...] += part

    @pl.when(step == pl.num_programs(0) * pl.num_programs(1) - 1)
    def _():
        row = lax.broadcasted_iota(jnp.int32, (rows, rows), 0)
        col = lax.broadcasted_iota(jnp.int32, (rows, rows), 1)
        kept = jnp.where(row % SUB == col % SUB, total[...], 0.0)
        slot = lax.broadcasted_iota(jnp.int32, (vectors, rows), 0)
        pick = (place[:1, :] == slot).astype(jnp.float32)
        half = jnp.dot(
            pick, kept, preferred_element_type=jnp.float32, precision=lax.Precision.HIGHEST
        )
        out[...] = lax.dot_general(
            half,
            pick,
            (((1,), (1,)), ((), ())),
            preferred_element_type=jnp.float32,
            precision=lax.Precision.HIGHEST,
        )


def gram_sums(specs, order, weight, waves):
    _, levels, slot_rows, degrees = specs[0].shape
    vectors = len(order)
    place = jnp.repeat(jnp.asarray(order, jnp.int32), SUB)
    place = jnp.broadcast_to(place[None], (SUB, vectors * SUB))
    return pl.pallas_call(
        functools.partial(gram_kernel, len(specs)),
        grid=(levels, slot_rows // SUB),
        in_specs=[
            pl.BlockSpec((s.shape[0], 1, SUB, degrees), lambda l, i: (0, l, i, 0)) for s in specs
        ]
        + [
            pl.BlockSpec((1, 1, degrees), lambda l, i: (l, 0, 0)),
            pl.BlockSpec((SUB, LANES), lambda l, i: (i, 0)),
            pl.BlockSpec((SUB, vectors * SUB), lambda l, i: (0, 0)),
        ],
        out_specs=pl.BlockSpec((vectors, vectors), lambda l, i: (0, 0)),
        out_shape=jax.ShapeDtypeStruct((vectors, vectors), jnp.float32),
        scratch_shapes=[pltpu.VMEM((vectors * SUB, vectors * SUB), jnp.float32)],
        compiler_params=pltpu.CompilerParams(vmem_limit_bytes=48 * 2**20),
        name="gram",
    )(*specs, weight.reshape(levels, 1, degrees), waves, place)


def chunk_sizes(half):
    ends = [2] if half > 12 else []
    tail = [2, 1] if half > 12 else []
    left = half - sum(ends) - sum(tail)
    middle = [4] * (left // 4) + ([left % 4] if left % 4 else [])
    return ends + middle + tail


def cosine(turn, total):
    turn = turn.astype(jnp.float32)
    quadrant = jnp.floor(turn * (4.0 / total) + 0.5)
    angle = (turn - quadrant * (total / 4.0)) * (2.0 * math.pi / total)
    square = angle * angle
    even = 1.0 + square * (-1 / 2 + square * (1 / 24 + square * (-1 / 720 + square / 40320)))
    odd = 1.0 + square * (-1 / 6 + square * (1 / 120 + square * (-1 / 5040 + square / 362880)))
    quadrant = quadrant.astype(jnp.int32)
    value = jnp.where(quadrant % 2 == 0, even, angle * odd)
    return jnp.where((quadrant + 1) % 4 < 2, value, -value)


def make_tables(wave_of_slot, bands, per_dev, lon_dev, lon_total):
    xs = lax.axis_size("x")
    my_x = lax.axis_index("x")
    my_core = lax.axis_index("core")
    waves = wave_of_slot.reshape(bands, xs, CORES * per_dev).transpose(1, 0, 2).reshape(xs, -1)
    waves = jnp.roll(waves, -my_x, axis=0)
    quarter = jnp.arange(waves.shape[1] * 2, dtype=jnp.int32) % 2 * (lon_total // 4)
    longitude = jnp.arange(lon_dev, dtype=jnp.int32)
    tables = []
    for core in (my_core, 1 - my_core):
        here = (my_x * CORES + core) * lon_dev + longitude
        tables.append(
            [
                cosine(
                    jnp.repeat(waves[step], 2)[:, None] * here[None, :] + quarter[:, None],
                    lon_total,
                ).astype(jnp.bfloat16)
                for step in range(xs)
            ]
        )
    return tables


def fast(grid_fields, legendre, wave_of_slot, energy_weight):
    lat_dev, vectors, levels, lon_dev = grid_fields.shape
    bands = lax.axis_size("lat")
    xs = lax.axis_size("x")
    lon_total = lon_dev * xs * CORES
    per_dev, _, degrees = legendre.shape
    slots = wave_of_slot.shape[0]
    scale = 1.0 / math.sqrt(lon_total)
    half = vectors // CORES
    my_core = lax.axis_index("core")
    by_field = grid_fields.transpose(1, 2, 0, 3).reshape(vectors * levels, lat_dev, lon_dev)
    swap = [(0, 1), (1, 0)]
    sizes = chunk_sizes(half)
    starts = [sum(sizes[:i]) for i in range(len(sizes))]

    tables = make_tables(wave_of_slot, bands, per_dev, lon_dev, lon_total)
    device_slot = lax.axis_index(("lat", "x", "core")) * per_dev
    own_waves = lax.dynamic_slice_in_dim(wave_of_slot, device_slot, per_dev, 0)
    wave_rows = jnp.broadcast_to(jnp.repeat(own_waves, 2)[:, None], (2 * per_dev, LANES))

    done = []
    order = []
    for count, offset in zip(sizes, starts, strict=True):
        rows = Rows(count * levels, lat_dev)

        def fields_of(core, offset=offset, rows=rows):
            first = (core * half + offset) * levels
            return lax.dynamic_slice_in_dim(by_field, first, rows.fields, 0)

        own = fields_of(my_core)
        came = lax.ppermute(fields_of(1 - my_core), "core", swap)
        add = None
        for step in range(1, xs):
            there = fourier(tables[0][step], tables[1][step], own, came, scale, rows)
            part = lax.ppermute(there, "x", [(j, (j + step) % xs) for j in range(xs)])
            add = part if xs == 2 else part.astype(jnp.float32) + (0.0 if add is None else add)
        mine = fourier(tables[0][0], tables[1][0], own, came, scale, rows, add)
        mine = mine.reshape(bands * CORES, 2 * per_dev, -1)
        cof = lax.all_to_all(mine, ("lat", "core"), 0, 0, tiled=True)
        sums = legendre_sums(cof, legendre, wave_rows, rows)
        done.append(sums.reshape(CORES * count, levels, 2 * per_dev, degrees))
        order += [c * half + offset + k for c in range(CORES) for k in range(count)]
    shape = (CORES, -1, levels, per_dev, 2, degrees)
    spectral = jnp.concatenate([d.reshape(shape) for d in done], axis=1)
    partial_value = gram_sums(done, order, energy_weight, wave_rows)
    parts = lax.all_gather(partial_value, ("lat", "x", "core"))
    gram_matrix = jnp.sum(parts, axis=0) / (levels * slots * degrees)
    return (spectral.reshape(vectors, levels, per_dev, 2, degrees), gram_matrix)


def on_device(grid_fields, legendre, wave_of_slot, energy_weight):
    lat_dev, vectors, _, lon_dev = grid_fields.shape
    bands = lax.axis_size("lat")
    rest = lat_dev % LANES
    fits = (
        lat_dev // LANES == 1
        and rest >= 16
        and LANES % rest == 0
        and bands % (LANES // rest) == 0
        and legendre.shape[0] * 2 % SUB == 0
        and vectors % CORES == 0
        and lon_dev % LANES == 0
    )
    body = fast if fits else plain
    return body(grid_fields, legendre, wave_of_slot, energy_weight)


def solution(mesh):
    lat, lon = mesh.devices.shape
    wide = Mesh(mesh.devices.reshape(lat, lon // CORES, CORES), ("lat", "x", "core"))
    lons = ("x", "core")
    placed = (P("lat", None, None, lons), P(("lat", "x", "core"), None, None), P(), P())
    return jax.shard_map(
        on_device,
        mesh=wide,
        in_specs=placed,
        out_specs=(P(None, None, ("lat", "x", "core"), None, None), P()),
        check_vma=False,
    )
```

time: 2210 us -> 646 us (0.29)
  blocking collectives: 955 us -> 44.8 us
  waiting for transfers between devices: 644 us -> 242 us
  local copies, waits for them, and re-layouts: 401 us -> 79.7 us
  Pallas kernels: 0 us -> 185 us
  matrix products: 132 us -> 0 us
  starting transfers between devices: 19.6 us -> 72.3 us
  other arithmetic: 39.7 us -> 11.3 us
    all_to_all x1 -> x0, blocking collectives: 916 us -> none  [on_device(): lax.all_to_all(fourier, 'lat', split_axis=2, concat_axis=0, tiled=True)]
    all_to_all x2 -> x8, waiting for transfers between devices: 644 us -> 0.02 us  [fast(): cof = lax.all_to_all(mine, ('lat', 'core'), 0, 0, tiled=True)]
    ppermute x0 -> x16, waiting for transfers between devices: none -> 242 us  [the longest x8 242 us: fast(): part = lax.ppermute(there, 'x', [(j, (j + step) % xs) for j in range(xs)])]
    pallas_call x0 -> x25, Pallas kernels: none -> 185 us  [the longest x8 95.1 us: legendre_sums(): pl.pallas_call(functools.partial(legendre_kernel, bands, rows, lat_dev, d...]
    all_to_all x4 -> x0, local copies, waits for them, and re-layouts: 138 us -> none  [the longest x2 64.6 us: on_device(): lax.all_to_all(fourier, 'lat', split_axis=2, concat_axis=0, tiled=True)]
    dot_general x3 -> x0, matrix products: 132 us -> none  [the longest x1 76.5 us: on_device(): jnp.einsum('aftp,tan->ftpn', columns, legendre_table, precision=lax.Preci...]
    mul x6 -> x2, local copies, waits for them, and re-layouts: 97 us -> 0.29 us  [make_tables(): jnp.repeat(waves[step], 2)[:, None] * here[None, :] + quarter[:, None]]
    transpose x2 -> x1, local copies, waits for them, and re-layouts: 61.7 us -> 0.01 us  [make_tables(): wave_of_slot.reshape(bands, xs, CORES * per_dev).transpose(1, 0, 2)]
  transfers between devices with their start and end apart: 2 -> 24, of which waited for: 2 -> 8; matrix products, arithmetic and copies ran while one was open for 2% -> 8% of each run, Pallas kernels for 0% -> 26%
where the time goes in v1:
time: 646 us; the launch traced here: 637 us
  waiting for transfers between devices  242 us (37%)
  Pallas kernels  185 us (29%)
  local copies, waits for them, and re-layouts  79.7 us (12%)
  starting transfers between devices  72.3 us (11%)
  blocking collectives  44.8 us (7%)
  other arithmetic  11.3 us (2%)
    ppermute x8, waiting for transfers between devices, fast(): part = lax.ppermute(there, 'x', [(j, (j + step) % xs) for j in range(xs)])  242 us
    pallas_call x8, Pallas kernels, legendre_sums(): pl.pallas_call(functools.partial(legendre_kernel, bands, rows, lat_dev, d...  95.1 us
    pallas_call x16, Pallas kernels, fourier(): pl.pallas_call(functools.partial(fourier_kernel, scale, rows, add is not...  80.7 us
    all_to_all x8, starting transfers between devices, fast(): cof = lax.all_to_all(mine, ('lat', 'core'), 0, 0, tiled=True)  57.7 us
    all_gather x1, blocking collectives, fast(): parts = lax.all_gather(partial_value, ('lat', 'x', 'core'))  44.8 us
    unnamed x89, local copies, waits for them, and re-layouts  32.2 us
    dynamic_slice x3, local copies, waits for them, and re-layouts, fields_of(): return lax.dynamic_slice_in_dim(by_field, first, rows.fields, 0)  23.5 us
    another operation x8, local copies, waits for them, and re-layouts, fast(): spectral = jnp.concatenate([d.reshape(shape) for d in done], axis=1)  21.4 us
  transfers between devices with their start and end apart: 24, of which 8 were waited for; matrix products, arithmetic and copies ran while one was open for 8% of the time, Pallas kernels for 26%

profile of v1, /device:TPU:0, one launch (start us, length us, event | category | flops | bytes accessed | tf_op | source)
XLA Modules:
  0.0 636.7 jit_solution(14869321048384273785)
XLA Ops:
  8.5 10.6 %fusion.14 = (bf16[512,640]{1,0:T(8,128)(2,1)S(1)}, bf16[512,640]{1,0:T(8,128)(2,1)S(1)}, bf16[512,640]{1,0:T(8,128)(2,1)S(1)}, bf16[512,640]{1,0:T(8,128)(2,1)S(1)}) fusion(s32[512]{0:T(512)S(1)} %mul.316, s32[512]{0:T(512)S(1)} %fusion.44, s32[640]{0:T(1024)S(1)} %get-tuple-element.27, s32[512]{0:T(512)S(1)} %mul.281, s32[640]{0:T(1024)S(1)} %get-tuple-element.26), kind=kLoop, calls=%fused_computation.42 | loop fusion | flops 74711040 | bytes 2632704 | tf_op jit(solution)/shard_map/convert_element_type | solution.py:319
  25.4 12.4 %collective-permute-done.15.refs_4_ = bf16[512,512]{1,0:T(8,128)(2,1)} collective-permute-done((bf16[512,512]{1,0:T(8,128)(2,1)}, bf16[512,512]{1,0:T(8,128)(2,1)}, u32[]{:S(2)}, u32[]{:S(2)}) %collective-permute-start.15) | collective-permute-done | bytes 524320 | tf_op jit(solution)/shard_map/ppermute | solution.py:360
  56.1 16.9 %constant_dynamic-slice_fusion.5 = (bf16[12,160,640]{2,1,0:T(8,128)(2,1)}, bf16[12,160,640]{2,1,0:T(8,128)(2,1)}, bf16[12,160,640]{2,1,0:T(8,128)(2,1)}, bf16[12...) fusion(bf16[150,160,640]{2,1,0:T(8,128)(2,1)} %bitcast.40, ...), kind=kLoop, calls=%fused_computation.118 | loop fusion | bytes 49152040 | tf_op jit(solution)/shard_map/dynamic_slice | solution.py:353
  73.6 6.8 %collective-permute-done.13.refs_4_ = bf16[512,1024]{1,0:T(8,128)(2,1)} collective-permute-done((bf16[512,1024]{1,0:T(8,128)(2,1)}, bf16[512,1024]{1,0:T(8,128)(2,1)}, u32[]{:S(2)}, u32[]{:S(2)}) %collective-permute-start.13) | collective-permute-done | bytes 1048608 | tf_op jit(solution)/shard_map/ppermute | solution.py:360
  84.8 16.2 %all-to-all-start.6 = ((bf16[16,32,1024]{2,1,0:T(8,128)(2,1)}), bf16[16,32,1024]{2,1,0:T(8,128)(2,1)}, u32[]{:S(2)}, u32[]{:S(2)}) async-start(bf16[16,32,1024]{2,1,0:T(8,128)(2,1)} %bitcast.33), calls=%async_computation.6 | async-start | bytes 2097152 | tf_op jit(solution)/shard_map/all_to_all | solution.py:364
  114.7 17.9 %collective-permute-done.1.refs_4_ = bf16[512,1024]{1,0:T(8,128)(2,1)S(1)} collective-permute-done((bf16[512,1024]{1,0:T(8,128)(2,1)S(1)}, bf16[512,1024]{1,0:T(8,128)(2,1)S(1)}, u32[]{:S(2)}, u32[]{:S(2)}) %collective-permute-start.1) | collective-permute-done | bytes 1048608 | tf_op jit(solution)/shard_map/ppermute | solution.py:360
  143.2 31.1 %collective-permute-done.11.refs_4_ = bf16[512,1920]{1,0:T(8,128)(2,1)} collective-permute-done((bf16[512,1920]{1,0:T(8,128)(2,1)}, bf16[512,1920]{1,0:T(8,128)(2,1)}, u32[]{:S(2)}, u32[]{:S(2)}) %collective-permute-start.11) | collective-permute-done | bytes 1966112 | tf_op jit(solution)/shard_map/ppermute | solution.py:360
  174.4 7.0 %fourier.27 = bf16[512,1920]{1,0:T(8,128)(2,1)} custom-call(bf16[512,640]{1,0:T(8,128)(2,1)S(1)} %get-tuple-element.21.refs_0_, bf16[512,640]{1,0:T(8,128)(2,1)S(1)} %get-tuple-element.22.refs_1_, bf16[12,160,640]{2,1,0:T(8,128)(2,1)} %get-tuple-element.9.refs_2_, bf16[12,160,640]{2,1,0:T(8,128)(2,1)} %collective-permute-done.10.refs_3_, ...), custom_call_target="tpu_custom_call" | custom-call | flops 2516582400 | bytes 10158080 | tf_op jit(solution)/shard_map/fourier/pallas_call | solution.py:129
  197.1 43.5 %collective-permute-done.9.refs_4_ = bf16[512,1920]{1,0:T(8,128)(2,1)S(1)} collective-permute-done((bf16[512,1920]{1,0:T(8,128)(2,1)S(1)}, bf16[512,1920]{1,0:T(8,128)(2,1)S(1)}, u32[]{:S(2)}, u32[]{:S(2)}) %collective-permute-start.9) | collective-permute-done | bytes 1966112 | tf_op jit(solution)/shard_map/ppermute | solution.py:360
  261.7 43.5 %collective-permute-done.7.refs_4_ = bf16[512,1920]{1,0:T(8,128)(2,1)S(1)} collective-permute-done((bf16[512,1920]{1,0:T(8,128)(2,1)S(1)}, bf16[512,1920]{1,0:T(8,128)(2,1)S(1)}, u32[]{:S(2)}, u32[]{:S(2)}) %collective-permute-start.7) | collective-permute-done | bytes 1966112 | tf_op jit(solution)/shard_map/ppermute | solution.py:360
  305.2 6.7 %fourier.23 = bf16[512,1920]{1,0:T(8,128)(2,1)} custom-call(bf16[512,640]{1,0:T(8,128)(2,1)S(1)} %get-tuple-element.21.refs_0_, bf16[512,640]{1,0:T(8,128)(2,1)S(1)} %get-tuple-element.22.refs_1_, bf16[12,160,640]{2,1,0:T(8,128)(2,1)} %get-tuple-element.13.refs_2_, bf16[12,160,640]{2,1,0:T(8,128)(2,1)} %collective-permute-done.6.refs_3_, ...), custom_call_target="tpu_custom_call" | custom-call | flops 2516582400 | bytes 10158080 | tf_op jit(solution)/shard_map/fourier/pallas_call | solution.py:129
  326.4 43.5 %collective-permute-done.5.refs_4_ = bf16[512,1920]{1,0:T(8,128)(2,1)S(1)} collective-permute-done((bf16[512,1920]{1,0:T(8,128)(2,1)S(1)}, bf16[512,1920]{1,0:T(8,128)(2,1)S(1)}, u32[]{:S(2)}, u32[]{:S(2)}) %collective-permute-start.5) | collective-permute-done | bytes 1966112 | tf_op jit(solution)/shard_map/ppermute | solution.py:360
  390.9 43.6 %collective-permute-done.3.refs_4_ = bf16[512,1920]{1,0:T(8,128)(2,1)S(1)} collective-permute-done((bf16[512,1920]{1,0:T(8,128)(2,1)S(1)}, bf16[512,1920]{1,0:T(8,128)(2,1)S(1)}, u32[]{:S(2)}, u32[]{:S(2)}) %collective-permute-start.3) | collective-permute-done | bytes 1966112 | tf_op jit(solution)/shard_map/ppermute | solution.py:360
  434.5 6.6 %fourier.19 = bf16[512,1920]{1,0:T(8,128)(2,1)} custom-call(bf16[512,640]{1,0:T(8,128)(2,1)S(1)} %get-tuple-element.21.refs_0_, bf16[512,640]{1,0:T(8,128)(2,1)S(1)} %get-tuple-element.22.refs_1_, bf16[12,160,640]{2,1,0:T(8,128)(2,1)} %get-tuple-element.17.refs_2_, bf16[12,160,640]{2,1,0:T(8,128)(2,1)} %collective-permute-done.2.refs_3_, ...), custom_call_target="tpu_custom_call" | custom-call | flops 2516582400 | bytes 10158080 | tf_op jit(solution)/shard_map/fourier/pallas_call | solution.py:129
  448.4 10.8 %legendre.15 = bf16[6,32,640]{2,1,0:T(8,128)(2,1)} custom-call(bf16[16,32,512]{2,1,0:T(8,128)(2,1)} %copy-done.35, bf16[16,1280,640]{2,1,0:T(8,128)(2,1)} %leg.15, s32[32,128]{1,0:T(8,128)} %broadcast_in_dim.40.wave.refs_9_), custom_call_target="tpu_custom_call" | custom-call | flops 629145600 | bytes 26738688 | tf_op jit(solution)/shard_map/legendre/pallas_call | solution.py:198
  460.9 11.1 %legendre.8 = bf16[12,32,640]{2,1,0:T(8,128)(2,1)} custom-call(bf16[16,32,1024]{2,1,0:T(8,128)(2,1)} %copy-done.29, bf16[16,1280,640]{2,1,0:T(8,128)(2,1)} %leg.15, s32[32,128]{1,0:T(8,128)} %broadcast_in_dim.40.wave.refs_9_), custom_call_target="tpu_custom_call" | custom-call | flops 1258291200 | bytes 27262976 | tf_op jit(solution)/shard_map/legendre/pallas_call | solution.py:198
  473.3 11.1 %legendre.14 = bf16[12,32,640]{2,1,0:T(8,128)(2,1)} custom-call(bf16[16,32,1024]{2,1,0:T(8,128)(2,1)} %all-to-all-done.6.cof, bf16[16,1280,640]{2,1,0:T(8,128)(2,1)} %leg.15, s32[32,128]{1,0:T(8,128)} %broadcast_in_dim.40.wave.refs_9_), custom_call_target="tpu_custom_call" | custom-call | flops 1258291200 | bytes 27262976 | tf_op jit(solution)/shard_map/legendre/pallas_call | solution.py:198
  487.5 12.4 %legendre.13 = bf16[24,32,640]{2,1,0:T(8,128)(2,1)} custom-call(bf16[16,32,1920]{2,1,0:T(8,128)(2,1)} %all-to-all-done.5.cof, bf16[16,1280,640]{2,1,0:T(8,128)(2,1)} %leg.15, s32[32,128]{1,0:T(8,128)} %broadcast_in_dim.40.wave.refs_9_), custom_call_target="tpu_custom_call" | custom-call | flops 2516582400 | bytes 28180480 | tf_op jit(solution)/shard_map/legendre/pallas_call | solution.py:198
  503.1 12.4 %legendre.12 = bf16[24,32,640]{2,1,0:T(8,128)(2,1)} custom-call(bf16[16,32,1920]{2,1,0:T(8,128)(2,1)} %all-to-all-done.4.cof, bf16[16,1280,640]{2,1,0:T(8,128)(2,1)} %leg.15, s32[32,128]{1,0:T(8,128)} %broadcast_in_dim.40.wave.refs_9_), custom_call_target="tpu_custom_call" | custom-call | flops 2516582400 | bytes 28180480 | tf_op jit(solution)/shard_map/legendre/pallas_call | solution.py:198
  518.7 12.4 %legendre.11 = bf16[24,32,640]{2,1,0:T(8,128)(2,1)} custom-call(bf16[16,32,1920]{2,1,0:T(8,128)(2,1)} %all-to-all-done.3.cof, bf16[16,1280,640]{2,1,0:T(8,128)(2,1)} %leg.15, s32[32,128]{1,0:T(8,128)} %broadcast_in_dim.40.wave.refs_9_), custom_call_target="tpu_custom_call" | custom-call | flops 2516582400 | bytes 28180480 | tf_op jit(solution)/shard_map/legendre/pallas_call | solution.py:198
  534.7 12.4 %legendre.10 = bf16[24,32,640]{2,1,0:T(8,128)(2,1)} custom-call(bf16[16,32,1920]{2,1,0:T(8,128)(2,1)} %all-to-all-done.2.cof, bf16[16,1280,640]{2,1,0:T(8,128)(2,1)} %leg.15, s32[32,128]{1,0:T(8,128)} %broadcast_in_dim.40.wave.refs_9_), custom_call_target="tpu_custom_call" | custom-call | flops 2516582400 | bytes 28180480 | tf_op jit(solution)/shard_map/legendre/pallas_call | solution.py:198
  551.5 12.5 %legendre.9 = bf16[24,32,640]{2,1,0:T(8,128)(2,1)} custom-call(bf16[16,32,1920]{2,1,0:T(8,128)(2,1)} %copy-done.28, bf16[16,1280,640]{2,1,0:T(8,128)(2,1)} %leg.15, s32[32,128]{1,0:T(8,128)} %broadcast_in_dim.40.wave.refs_9_), custom_call_target="tpu_custom_call" | custom-call | flops 2516582400 | bytes 28180480 | tf_op jit(solution)/shard_map/legendre/pallas_call | solution.py:198
  571.8 9.2 %gram.1 = f32[50,50]{1,0:T(8,128)S(1)} custom-call(bf16[4,3,32,640]{3,2,1,0:T(8,128)(2,1)S(1)} %bitcast.31, bf16[8,3,32,640]{3,2,1,0:T(8,128)(2,1)S(1)} %bitcast.30, bf16[8,3,32,640]{3,2,1,0:T(8,128)(2,1)S(1)} %bitcast.29, bf16[8,3,32,640]{3,2,1,0:T(8,128)(2,1)S(1)} %bitcast.28, bf16[8,3,32,640]{3,2,1,0:T(8,128)(2,1)S(1)} %bitcast.27, ...), custom_call_target="tpu_custom_call" | custom-call | tf_op jit(solution)/shard_map/gram/pallas_call | solution.py:264
  581.0 44.8 %all-gather.1 = f32[32,50,50]{2,1,0:T(8,128)S(1)} all-gather(f32[1,50,50]{2,1,0:T(8,128)S(1)} %bitcast.37), channel_id=2, replica_groups=mesh['lat'=8,'x'=2,'core'=2] {'lat','x','core'}, dimensions={0}, use_global_device_ids=true | all-gather | bytes 330000 | tf_op jit(solution)/shard_map/all_gather | solution.py:371
  (173 shorter events, 179.9 us)
Async XLA Ops:
  5.0 42.0 %collective-permute-start.12 = (bf16[6,160,640]{2,1,0:T(8,128)(2,1)}, bf16[6,160,640]{2,1,0:T(8,128)(2,1)}, u32[]{:S(2)}, u32[]{:S(2)}) collective-permute-start(bf16[6,160,640]{2,1,0:T(8,128)(2,1)} %get-tuple-element.4), channel_id=1, source_target_pairs={{0,1},{1,0},{2,3},{3,2},{4,5},{5,4},{6,7},{7,6},{8,9},{9,8},{10,11... | collective-permute-start | bytes 3686408 | tf_op jit(solution)/shard_map/ppermute | solution.py:356
  7.7 11.4 %collective-permute-start.14 = (bf16[3,160,640]{2,1,0:T(8,128)(2,1)}, bf16[3,160,640]{2,1,0:T(8,128)(2,1)}, u32[]{:S(2)}, u32[]{:S(2)}) collective-permute-start(bf16[3,160,640]{2,1,0:T(8,128)(2,1)} %get-tuple-element.2), channel_id=1, source_target_pairs={{0,1},{1,0},{2,3},{3,2},{4,5},{5,4},{6,7},{7,6},{8,9},{9,8},{10,11... | collective-permute-start | bytes 1843208 | tf_op jit(solution)/shard_map/ppermute | solution.py:356
  22.5 15.4 %collective-permute-start.15 = (bf16[512,512]{1,0:T(8,128)(2,1)}, bf16[512,512]{1,0:T(8,128)(2,1)}, u32[]{:S(2)}, u32[]{:S(2)}) collective-permute-start(bf16[512,512]{1,0:T(8,128)(2,1)} %fourier.30), channel_id=1, source_target_pairs={{0,2},{2,0},{1,3},{3,1},{4,6},{6,4},{5,7},{7,5},{8,10},{10,8},{9,1... | collective-permute-start | bytes 1572872 | tf_op jit(solution)/shard_map/ppermute | solution.py:360
  40.9 44.0 %all-to-all-start.7 = ((bf16[16,32,512]{2,1,0:T(8,128)(2,1)}), bf16[16,32,512]{2,1,0:T(8,128)(2,1)S(1)}, u32[]{:S(2)}, u32[]{:S(2)}) async-start(bf16[16,32,512]{2,1,0:T(8,128)(2,1)} %bitcast.36), calls=%async_computation.7 | async-start | bytes 1048576 | tf_op jit(solution)/shard_map/all_to_all | solution.py:364
  54.6 25.8 %collective-permute-start.13 = (bf16[512,1024]{1,0:T(8,128)(2,1)}, bf16[512,1024]{1,0:T(8,128)(2,1)}, u32[]{:S(2)}, u32[]{:S(2)}) collective-permute-start(bf16[512,1024]{1,0:T(8,128)(2,1)} %fourier.28), channel_id=1, source_target_pairs={{0,2},{2,0},{1,3},{3,1},{4,6},{6,4},{5,7},{7,5},{8,10},{10,8},{9,1... | collective-permute-start | bytes 3145736 | tf_op jit(solution)/shard_map/ppermute | solution.py:360
  73.0 35.0 %collective-permute-start.10 = (bf16[12,160,640]{2,1,0:T(8,128)(2,1)}, bf16[12,160,640]{2,1,0:T(8,128)(2,1)}, u32[]{:S(2)}, u32[]{:S(2)}) collective-permute-start(bf16[12,160,640]{2,1,0:T(8,128)(2,1)} %get-tuple-element.8), channel_id=1, source_target_pairs={{0,1},{1,0},{2,3},{3,2},{4,5},{5,4},{6,7},{7,6},{8,9},{9,8},{10,11... | collective-permute-start | bytes 7372808 | tf_op jit(solution)/shard_map/ppermute | solution.py:356
  73.2 27.8 %collective-permute-start = (bf16[6,160,640]{2,1,0:T(8,128)(2,1)}, bf16[6,160,640]{2,1,0:T(8,128)(2,1)}, u32[]{:S(2)}, u32[]{:S(2)}) collective-permute-start(bf16[6,160,640]{2,1,0:T(8,128)(2,1)} %get-tuple-element.6), channel_id=1, source_target_pairs={{0,1},{1,0},{2,3},{3,2},{4,5},{5,4},{6,7},{7,6},{8,9},{9,8},{10,11... | collective-permute-start | bytes 3686408 | tf_op jit(solution)/shard_map/ppermute | solution.py:356
  84.8 51.9 %all-to-all-start.6 = ((bf16[16,32,1024]{2,1,0:T(8,128)(2,1)}), bf16[16,32,1024]{2,1,0:T(8,128)(2,1)}, u32[]{:S(2)}, u32[]{:S(2)}) async-start(bf16[16,32,1024]{2,1,0:T(8,128)(2,1)} %bitcast.33), calls=%async_computation.6 | async-start | bytes 2097152 | tf_op jit(solution)/shard_map/all_to_all | solution.py:364
  106.5 26.1 %collective-permute-start.1 = (bf16[512,1024]{1,0:T(8,128)(2,1)S(1)}, bf16[512,1024]{1,0:T(8,128)(2,1)S(1)}, u32[]{:S(2)}, u32[]{:S(2)}) collective-permute-start(bf16[512,1024]{1,0:T(8,128)(2,1)S(1)} %fourier.16), channel_id=1, source_target_pairs={{0,2},{2,0},{1,3},{3,1},{4,6},{6,4},{5,7},{7,5},{8,10},{10,8},{9,1... | collective-permute-start | bytes 3145736 | tf_op jit(solution)/shard_map/ppermute | solution.py:360
  114.2 60.2 %collective-permute-start.11 = (bf16[512,1920]{1,0:T(8,128)(2,1)}, bf16[512,1920]{1,0:T(8,128)(2,1)}, u32[]{:S(2)}, u32[]{:S(2)}) collective-permute-start(bf16[512,1920]{1,0:T(8,128)(2,1)} %fourier.26), channel_id=1, source_target_pairs={{0,2},{2,0},{1,3},{3,1},{4,6},{6,4},{5,7},{7,5},{8,10},{10,8},{9,1... | collective-permute-start | bytes 5898248 | tf_op jit(solution)/shard_map/ppermute | solution.py:360
  136.7 44.7 %all-to-all-start = ((bf16[16,32,1024]{2,1,0:T(8,128)(2,1)}), bf16[16,32,1024]{2,1,0:T(8,128)(2,1)S(1)}, u32[]{:S(2)}, u32[]{:S(2)}) async-start(bf16[16,32,1024]{2,1,0:T(8,128)(2,1)} %bitcast.34), calls=%async_computation | async-start | bytes 2097152 | tf_op jit(solution)/shard_map/all_to_all | solution.py:364
  142.8 45.5 %collective-permute-start.8 = (bf16[12,160,640]{2,1,0:T(8,128)(2,1)}, bf16[12,160,640]{2,1,0:T(8,128)(2,1)}, u32[]{:S(2)}, u32[]{:S(2)}) collective-permute-start(bf16[12,160,640]{2,1,0:T(8,128)(2,1)} %get-tuple-element.10), channel_id=1, source_target_pairs={{0,1},{1,0},{2,3},{3,2},{4,5},{5,4},{6,7},{7,6},{8,9},{9,8},{10,11... | collective-permute-start | bytes 7372808 | tf_op jit(solution)/shard_map/ppermute | solution.py:356
  182.4 64.8 %all-to-all-start.5 = ((bf16[16,32,1920]{2,1,0:T(8,128)(2,1)}), bf16[16,32,1920]{2,1,0:T(8,128)(2,1)}, u32[]{:S(2)}, u32[]{:S(2)}) async-start(bf16[16,32,1920]{2,1,0:T(8,128)(2,1)} %bitcast.11), calls=%async_computation.5 | async-start | bytes 3932160 | tf_op jit(solution)/shard_map/all_to_all | solution.py:364
  195.4 45.2 %collective-permute-start.9 = (bf16[512,1920]{1,0:T(8,128)(2,1)S(1)}, bf16[512,1920]{1,0:T(8,128)(2,1)S(1)}, u32[]{:S(2)}, u32[]{:S(2)}) collective-permute-start(bf16[512,1920]{1,0:T(8,128)(2,1)S(1)} %fourier.24), channel_id=1, source_target_pairs={{0,2},{2,0},{1,3},{3,1},{4,6},{6,4},{5,7},{7,5},{8,10},{10,8},{9,1... | collective-permute-start | bytes 5898248 | tf_op jit(solution)/shard_map/ppermute | solution.py:360
  197.0 55.9 %collective-permute-start.6 = (bf16[12,160,640]{2,1,0:T(8,128)(2,1)}, bf16[12,160,640]{2,1,0:T(8,128)(2,1)}, u32[]{:S(2)}, u32[]{:S(2)}) collective-permute-start(bf16[12,160,640]{2,1,0:T(8,128)(2,1)} %get-tuple-element.12), channel_id=1, source_target_pairs={{0,1},{1,0},{2,3},{3,2},{4,5},{5,4},{6,7},{7,6},{8,9},{9,8},{10,11... | collective-permute-start | bytes 7372808 | tf_op jit(solution)/shard_map/ppermute | solution.py:356
  247.2 64.7 %all-to-all-start.4 = ((bf16[16,32,1920]{2,1,0:T(8,128)(2,1)}), bf16[16,32,1920]{2,1,0:T(8,128)(2,1)}, u32[]{:S(2)}, u32[]{:S(2)}) async-start(bf16[16,32,1920]{2,1,0:T(8,128)(2,1)} %bitcast.10), calls=%async_computation.4 | async-start | bytes 3932160 | tf_op jit(solution)/shard_map/all_to_all | solution.py:364
  260.0 45.1 %collective-permute-start.7 = (bf16[512,1920]{1,0:T(8,128)(2,1)S(1)}, bf16[512,1920]{1,0:T(8,128)(2,1)S(1)}, u32[]{:S(2)}, u32[]{:S(2)}) collective-permute-start(bf16[512,1920]{1,0:T(8,128)(2,1)S(1)} %fourier.22), channel_id=1, source_target_pairs={{0,2},{2,0},{1,3},{3,1},{4,6},{6,4},{5,7},{7,5},{8,10},{10,8},{9,1... | collective-permute-start | bytes 5898248 | tf_op jit(solution)/shard_map/ppermute | solution.py:360
  261.6 56.1 %collective-permute-start.4 = (bf16[12,160,640]{2,1,0:T(8,128)(2,1)}, bf16[12,160,640]{2,1,0:T(8,128)(2,1)}, u32[]{:S(2)}, u32[]{:S(2)}) collective-permute-start(bf16[12,160,640]{2,1,0:T(8,128)(2,1)} %get-tuple-element.14), channel_id=1, source_target_pairs={{0,1},{1,0},{2,3},{3,2},{4,5},{5,4},{6,7},{7,6},{8,9},{9,8},{10,11... | collective-permute-start | bytes 7372808 | tf_op jit(solution)/shard_map/ppermute | solution.py:356
  311.9 64.6 %all-to-all-start.3 = ((bf16[16,32,1920]{2,1,0:T(8,128)(2,1)}), bf16[16,32,1920]{2,1,0:T(8,128)(2,1)}, u32[]{:S(2)}, u32[]{:S(2)}) async-start(bf16[16,32,1920]{2,1,0:T(8,128)(2,1)} %bitcast.9), calls=%async_computation.3 | async-start | bytes 3932160 | tf_op jit(solution)/shard_map/all_to_all | solution.py:364
  324.8 45.1 %collective-permute-start.5 = (bf16[512,1920]{1,0:T(8,128)(2,1)S(1)}, bf16[512,1920]{1,0:T(8,128)(2,1)S(1)}, u32[]{:S(2)}, u32[]{:S(2)}) collective-permute-start(bf16[512,1920]{1,0:T(8,128)(2,1)S(1)} %fourier.20), channel_id=1, source_target_pairs={{0,2},{2,0},{1,3},{3,1},{4,6},{6,4},{5,7},{7,5},{8,10},{10,8},{9,1... | collective-permute-start | bytes 5898248 | tf_op jit(solution)/shard_map/ppermute | solution.py:360
  326.3 55.9 %collective-permute-start.2 = (bf16[12,160,640]{2,1,0:T(8,128)(2,1)}, bf16[12,160,640]{2,1,0:T(8,128)(2,1)}, u32[]{:S(2)}, u32[]{:S(2)}) collective-permute-start(bf16[12,160,640]{2,1,0:T(8,128)(2,1)} %get-tuple-element.16), channel_id=1, source_target_pairs={{0,1},{1,0},{2,3},{3,2},{4,5},{5,4},{6,7},{7,6},{8,9},{9,8},{10,11... | collective-permute-start | bytes 7372808 | tf_op jit(solution)/shard_map/ppermute | solution.py:356
  376.5 64.7 %all-to-all-start.2 = ((bf16[16,32,1920]{2,1,0:T(8,128)(2,1)}), bf16[16,32,1920]{2,1,0:T(8,128)(2,1)}, u32[]{:S(2)}, u32[]{:S(2)}) async-start(bf16[16,32,1920]{2,1,0:T(8,128)(2,1)} %bitcast.8), calls=%async_computation.2 | async-start | bytes 3932160 | tf_op jit(solution)/shard_map/all_to_all | solution.py:364
  389.4 45.1 %collective-permute-start.3 = (bf16[512,1920]{1,0:T(8,128)(2,1)S(1)}, bf16[512,1920]{1,0:T(8,128)(2,1)S(1)}, u32[]{:S(2)}, u32[]{:S(2)}) collective-permute-start(bf16[512,1920]{1,0:T(8,128)(2,1)S(1)} %fourier.18), channel_id=1, source_target_pairs={{0,2},{2,0},{1,3},{3,1},{4,6},{6,4},{5,7},{7,5},{8,10},{10,8},{9,1... | collective-permute-start | bytes 5898248 | tf_op jit(solution)/shard_map/ppermute | solution.py:360
  441.2 109.0 %all-to-all-start.1 = ((bf16[16,32,1920]{2,1,0:T(8,128)(2,1)}), bf16[16,32,1920]{2,1,0:T(8,128)(2,1)S(1)}, u32[]{:S(2)}, u32[]{:S(2)}) async-start(bf16[16,32,1920]{2,1,0:T(8,128)(2,1)} %bitcast.7), calls=%async_computation.1 | async-start | bytes 3932160 | tf_op jit(solution)/shard_map/all_to_all | solution.py:364
  (41 other events, 212.0 us)

commit v2 on v1

--- a/solution.py
+++ b/solution.py
@@ -13,6 +13,7 @@
 CORES = 2
 LANES = 128
 SUB = 8
+VMEM = 58 * 2**20
 
 
 def make_trig(wave_list, lon_total):
@@ -96,53 +97,59 @@
         return f // self.block * self.quads_in + inner // self.pack, inner % self.pack
 
 
-def fourier_kernel(scale, rows, with_add, *refs):
+def fourier_kernel(scale, rows, with_add, first, *refs):
+    own = refs[: rows.block]
     if with_add:
-        t0, t1, g0, g1, add, out = refs
+        t0, t1, other, add, out = refs[rows.block :]
     else:
-        t0, t1, g0, g1, out = refs
-
-    def packed(g):
-        parts = [g[f, :LANES, :] for f in range(rows.block)]
-        parts += [g[f, LANES:, :] for f in range(rows.block)]
-        spare = rows.width - rows.block * g.shape[1]
-        if spare:
-            parts.append(jnp.zeros((spare, g.shape[2]), g.dtype))
-        return jnp.concatenate(parts, axis=0)
-
+        t0, t1, other, out = refs[rows.block :]
+    spare = rows.width - rows.block * other.shape[1]
+    zero = [jnp.zeros((spare, other.shape[2]), other.dtype)] if spare else []
+    whole = range(rows.block)
+    g0 = [own[f][0, :LANES, :] for f in whole] + [own[f][0, LANES:, :] for f in whole]
+    g1 = [other[f, :LANES, :] for f in whole] + [other[f, LANES:, :] for f in whole]
     dims = (((1,), (1,)), ((), ()))
-    total = lax.dot_general(t0[...], packed(g0), dims, preferred_element_type=jnp.float32)
-    total += lax.dot_general(t1[...], packed(g1), dims, preferred_element_type=jnp.float32)
+    g0 = jnp.concatenate(g0 + zero, axis=0)
+    g1 = jnp.concatenate(g1 + zero, axis=0)
+    total = lax.dot_general(t0[...], g0, dims, preferred_element_type=jnp.float32)
+    total += lax.dot_general(t1[...], g1, dims, preferred_element_type=jnp.float32)
     total *= scale
     if with_add:
         total += add[...].astype(jnp.float32)
     out[...] = total.astype(out.dtype)
 
 
-def fourier(t0, t1, g0, g1, scale, rows, add=None):
+def fourier(t0, t1, by_field, first, other, scale, rows, add=None):
     cols, lon = t0.shape
-    lat_dev = g0.shape[1]
-    table = pl.BlockSpec((cols, lon), lambda i: (0, 0))
-    field = pl.BlockSpec((rows.block, lat_dev, lon), lambda i: (i, 0, 0))
-    wide = pl.BlockSpec((cols, rows.width), lambda i: (0, i))
-    args = [t0, t1, g0, g1] + ([] if add is None else [add])
+    lat_dev = other.shape[1]
+    table = pl.BlockSpec((cols, lon), lambda i, at: (0, 0))
+    own = [
+        pl.BlockSpec((1, lat_dev, lon), lambda i, at, f=f: (at[0] + i * rows.block + f, 0, 0))
+        for f in range(rows.block)
+    ]
+    field = pl.BlockSpec((rows.block, lat_dev, lon), lambda i, at: (i, 0, 0))
+    wide = pl.BlockSpec((cols, rows.width), lambda i, at: (0, i))
+    adds = [] if add is None else [add]
     return pl.pallas_call(
         functools.partial(fourier_kernel, scale, rows, add is not None),
-        grid=(rows.blocks,),
-        in_specs=[table, table, field, field] + ([] if add is None else [wide]),
-        out_specs=wide,
+        grid_spec=pltpu.PrefetchScalarGridSpec(
+            num_scalar_prefetch=1,
+            grid=(rows.blocks,),
+            in_specs=own + [table, table, field] + [wide for _ in adds],
+            out_specs=wide,
+        ),
         out_shape=jax.ShapeDtypeStruct((cols, rows.total), jnp.bfloat16),
-        compiler_params=pltpu.CompilerParams(vmem_limit_bytes=48 * 2**20),
+        compiler_params=pltpu.CompilerParams(vmem_limit_bytes=VMEM),
         cost_estimate=pl.CostEstimate(
             flops=4 * cols * rows.total * lon,
             bytes_accessed=4 * rows.total * lon + 4 * cols * rows.total + 4 * cols * lon,
             transcendentals=0,
         ),
         name="fourier",
-    )(*args)
-
-
-def legendre_kernel(bands, rows, lat_dev, degrees, cof, leg, wave, out):
+    )(first.reshape(1), *[by_field] * rows.block, t0, t1, other, *adds)
+
+
+def left_rows(bands, rows, cof):
     fields, pack, rest = rows.fields, rows.pack, rows.rest
     lane = lax.broadcasted_iota(jnp.int32, (CORES * rows.quads * SUB, LANES), 1) // rest
 
@@ -170,8 +177,16 @@
                 at = (c * rows.quads + quad) * SUB
                 pieces.append(shards[j][at : at + SUB])
         left.append(jnp.concatenate(pieces, axis=0))
-    count = CORES * fields * SUB
-    left = jnp.concatenate(left, axis=1)
+    return jnp.concatenate(left, axis=1)
+
+
+def legendre_kernel(bands, chunks, lat_dev, degrees, *refs):
+    cofs = refs[: len(chunks)]
+    leg, wave = refs[len(chunks) : len(chunks) + 2]
+    outs = refs[len(chunks) + 2 :]
+    left = [left_rows(bands, rows, cof) for rows, cof in zip(chunks, cofs, strict=True)]
+    left = jnp.concatenate(left, axis=0)
+    count = left.shape[0]
     slot_of_row = lax.broadcasted_iota(jnp.int32, (count, 1), 0) % SUB // 2
     total = jnp.zeros((count, degrees), jnp.float32)
     for s in range(SUB // 2):
@@ -182,37 +197,41 @@
             axis=0,
         )
         total += jnp.dot(here, table, preferred_element_type=jnp.float32)
-    total = total.reshape(CORES * fields, SUB, degrees)
+    total = total.reshape(count // SUB, SUB, degrees)
     degree = lax.broadcasted_iota(jnp.int32, (SUB, degrees), 1)
     keep = degree >= wave[:, :1]
     total = jnp.where(keep[None], total, 0.0)
-    out[...] = total.astype(out.dtype)
-
-
-def legendre_sums(cof, leg, waves, rows):
-    sources, slot_rows, _ = cof.shape
-    fields = rows.fields
+    at = 0
+    for out in outs:
+        out[...] = total[at : at + out.shape[0]].astype(out.dtype)
+        at += out.shape[0]
+
+
+def legendre_sums(cofs, chunks, leg, waves):
+    sources, slot_rows, _ = cofs[0].shape
     slots, lats, degrees = leg.shape
     bands = sources // CORES
     lat_dev = lats // bands
+    counts = [CORES * rows.fields for rows in chunks]
+    total = sum(rows.total for rows in chunks)
     return pl.pallas_call(
-        functools.partial(legendre_kernel, bands, rows, lat_dev, degrees),
+        functools.partial(legendre_kernel, bands, chunks, lat_dev, degrees),
         grid=(slot_rows // SUB,),
-        in_specs=[
-            pl.BlockSpec((sources, SUB, rows.total), lambda i: (0, i, 0)),
+        in_specs=[pl.BlockSpec((sources, SUB, rows.total), lambda i: (0, i, 0)) for rows in chunks]
+        + [
             pl.BlockSpec((SUB // 2, lats, degrees), lambda i: (i, 0, 0)),
             pl.BlockSpec((SUB, LANES), lambda i: (i, 0)),
         ],
-        out_specs=pl.BlockSpec((CORES * fields, SUB, degrees), lambda i: (0, i, 0)),
-        out_shape=jax.ShapeDtypeStruct((CORES * fields, slot_rows, degrees), jnp.bfloat16),
-        compiler_params=pltpu.CompilerParams(vmem_limit_bytes=56 * 2**20),
+        out_specs=[pl.BlockSpec((n, SUB, degrees), lambda i: (0, i, 0)) for n in counts],
+        out_shape=[jax.ShapeDtypeStruct((n, slot_rows, degrees), jnp.bfloat16) for n in counts],
+        compiler_params=pltpu.CompilerParams(vmem_limit_bytes=VMEM),
         cost_estimate=pl.CostEstimate(
-            flops=4 * CORES * fields * slot_rows * lats * degrees,
-            bytes_accessed=2 * sources * slot_rows * rows.total + 2 * slots * lats * degrees,
+            flops=4 * sum(counts) * slot_rows * lats * degrees,
+            bytes_accessed=2 * sources * slot_rows * total + 2 * slots * lats * degrees,
             transcendentals=0,
         ),
         name="legendre",
-    )(cof, leg, waves)
+    )(*cofs, leg, waves)
 
 
 def gram_kernel(groups, *refs):
@@ -275,52 +294,50 @@
         out_specs=pl.BlockSpec((vectors, vectors), lambda l, i: (0, 0)),
         out_shape=jax.ShapeDtypeStruct((vectors, vectors), jnp.float32),
         scratch_shapes=[pltpu.VMEM((vectors * SUB, vectors * SUB), jnp.float32)],
-        compiler_params=pltpu.CompilerParams(vmem_limit_bytes=48 * 2**20),
+        compiler_params=pltpu.CompilerParams(vmem_limit_bytes=VMEM),
         name="gram",
     )(*specs, weight.reshape(levels, 1, degrees), waves, place)
 
 
-def chunk_sizes(half):
-    ends = [2] if half > 12 else []
-    tail = [2, 1] if half > 12 else []
-    left = half - sum(ends) - sum(tail)
-    middle = [4] * (left // 4) + ([left % 4] if left % 4 else [])
-    return ends + middle + tail
+def chunk_sizes(half, quad):
+    first = half % quad
+    return ([first] if first else []) + [quad] * (half // quad)
+
+
+def groups_of(count):
+    pairs = [list(range(i, min(i + 2, count - 1))) for i in range(0, count - 1, 2)]
+    return pairs + [[count - 1]]
 
 
 def cosine(turn, total):
-    turn = turn.astype(jnp.float32)
-    quadrant = jnp.floor(turn * (4.0 / total) + 0.5)
-    angle = (turn - quadrant * (total / 4.0)) * (2.0 * math.pi / total)
+    inside = turn - jnp.floor(turn * (1.0 / total) + 0.5) * total
+    angle = inside * (2.0 * math.pi / total)
     square = angle * angle
-    even = 1.0 + square * (-1 / 2 + square * (1 / 24 + square * (-1 / 720 + square / 40320)))
-    odd = 1.0 + square * (-1 / 6 + square * (1 / 120 + square * (-1 / 5040 + square / 362880)))
-    quadrant = quadrant.astype(jnp.int32)
-    value = jnp.where(quadrant % 2 == 0, even, angle * odd)
-    return jnp.where((quadrant + 1) % 4 < 2, value, -value)
-
-
-def make_tables(wave_of_slot, bands, per_dev, lon_dev, lon_total):
-    xs = lax.axis_size("x")
-    my_x = lax.axis_index("x")
-    my_core = lax.axis_index("core")
-    waves = wave_of_slot.reshape(bands, xs, CORES * per_dev).transpose(1, 0, 2).reshape(xs, -1)
-    waves = jnp.roll(waves, -my_x, axis=0)
-    quarter = jnp.arange(waves.shape[1] * 2, dtype=jnp.int32) % 2 * (lon_total // 4)
-    longitude = jnp.arange(lon_dev, dtype=jnp.int32)
-    tables = []
-    for core in (my_core, 1 - my_core):
-        here = (my_x * CORES + core) * lon_dev + longitude
-        tables.append(
-            [
-                cosine(
-                    jnp.repeat(waves[step], 2)[:, None] * here[None, :] + quarter[:, None],
-                    lon_total,
-                ).astype(jnp.bfloat16)
-                for step in range(xs)
-            ]
-        )
-    return tables
+    value = 1.0 / math.factorial(18)
+    for k in range(8, -1, -1):
+        value = 1.0 / math.factorial(2 * k) - square * value
+    return value
+
+
+def make_tables(waves, here, lon_total):
+    part = jnp.arange(waves.shape[0] * 2, dtype=jnp.int32) % 2
+    quarter = part.astype(jnp.float32) * (lon_total / 4.0)
+    turn = jnp.repeat(waves, 2).astype(jnp.float32)[:, None] * here[None, :] + quarter[:, None]
+    return cosine(turn, float(lon_total)).astype(jnp.bfloat16)
+
+
+def all_sum(value):
+    for axis in ("core", "x", "lat"):
+        size = lax.axis_size(axis)
+        step = 1
+        while step < size:
+            value = value + lax.ppermute(value, axis, [(i, i ^ step) for i in range(size)])
+            step *= 2
+    return value
+
+
+def after(value, other):
+    return lax.optimization_barrier((value, other))[0]
 
 
 def fast(grid_fields, legendre, wave_of_slot, energy_weight):
@@ -333,43 +350,69 @@
     scale = 1.0 / math.sqrt(lon_total)
     half = vectors // CORES
     my_core = lax.axis_index("core")
+    my_x = lax.axis_index("x")
     by_field = grid_fields.transpose(1, 2, 0, 3).reshape(vectors * levels, lat_dev, lon_dev)
     swap = [(0, 1), (1, 0)]
-    sizes = chunk_sizes(half)
+    pack = LANES // (lat_dev % LANES)
+    sizes = chunk_sizes(half, pack // math.gcd(pack, levels))
     starts = [sum(sizes[:i]) for i in range(len(sizes))]
-
-    tables = make_tables(wave_of_slot, bands, per_dev, lon_dev, lon_total)
+    chunks = [Rows(size * levels, lat_dev) for size in sizes]
+    groups = groups_of(len(sizes))
+
+    waves = wave_of_slot.reshape(bands, xs, CORES * per_dev).transpose(1, 0, 2).reshape(xs, -1)
+    waves = jnp.roll(waves, -my_x, axis=0)
+    longitude = jnp.arange(lon_dev, dtype=jnp.int32)
+    sectors = [
+        ((my_x * CORES + core) * lon_dev + longitude).astype(jnp.float32)
+        for core in (my_core, 1 - my_core)
+    ]
+    tables = {s: [make_tables(waves[s], here, lon_total) for here in sectors] for s in range(1, xs)}
     device_slot = lax.axis_index(("lat", "x", "core")) * per_dev
     own_waves = lax.dynamic_slice_in_dim(wave_of_slot, device_slot, per_dev, 0)
     wave_rows = jnp.broadcast_to(jnp.repeat(own_waves, 2)[:, None], (2 * per_dev, LANES))
 
-    done = []
-    order = []
-    for count, offset in zip(sizes, starts, strict=True):
-        rows = Rows(count * levels, lat_dev)
-
-        def fields_of(core, offset=offset, rows=rows):
-            first = (core * half + offset) * levels
-            return lax.dynamic_slice_in_dim(by_field, first, rows.fields, 0)
-
-        own = fields_of(my_core)
-        came = lax.ppermute(fields_of(1 - my_core), "core", swap)
+    sent = []
+    cofs = []
+    done = {}
+    for i, rows in enumerate(chunks):
+        first = (my_core * half + starts[i]) * levels
+        away = ((1 - my_core) * half + starts[i]) * levels
+        if sent:
+            away = after(away, sent[max(i - 2, 0)])
+        away = lax.dynamic_slice_in_dim(by_field, away, rows.fields, 0)
+        came = lax.ppermute(away, "core", swap)
         add = None
         for step in range(1, xs):
-            there = fourier(tables[0][step], tables[1][step], own, came, scale, rows)
+            there = fourier(*tables[step], by_field, first, came, scale, rows)
             part = lax.ppermute(there, "x", [(j, (j + step) % xs) for j in range(xs)])
             add = part if xs == 2 else part.astype(jnp.float32) + (0.0 if add is None else add)
-        mine = fourier(tables[0][0], tables[1][0], own, came, scale, rows, add)
+        if not sent:
+            own_set = after(waves[0], there)
+            tables[0] = [make_tables(own_set, here, lon_total) for here in sectors]
+        sent.append(there)
+        mine = fourier(*tables[0], by_field, first, came, scale, rows, add)
         mine = mine.reshape(bands * CORES, 2 * per_dev, -1)
-        cof = lax.all_to_all(mine, ("lat", "core"), 0, 0, tiled=True)
-        sums = legendre_sums(cof, legendre, wave_rows, rows)
-        done.append(sums.reshape(CORES * count, levels, 2 * per_dev, degrees))
-        order += [c * half + offset + k for c in range(CORES) for k in range(count)]
+        if cofs:
+            mine = after(mine, cofs[-1])
+        cofs.append(lax.all_to_all(mine, ("lat", "core"), 0, 0, tiled=True))
+        for group in groups:
+            if group[-1] == i:
+                sums = legendre_sums(
+                    [cofs[j] for j in group], [chunks[j] for j in group], legendre, wave_rows
+                )
+                for j, value in zip(group, sums, strict=True):
+                    done[j] = value.reshape(-1, levels, 2 * per_dev, degrees)
+    done = [done[i] for i in range(len(chunks))]
+    order = [
+        c * half + start + k
+        for size, start in zip(sizes, starts, strict=True)
+        for c in range(CORES)
+        for k in range(size)
+    ]
     shape = (CORES, -1, levels, per_dev, 2, degrees)
     spectral = jnp.concatenate([d.reshape(shape) for d in done], axis=1)
     partial_value = gram_sums(done, order, energy_weight, wave_rows)
-    parts = lax.all_gather(partial_value, ("lat", "x", "core"))
-    gram_matrix = jnp.sum(parts, axis=0) / (levels * slots * degrees)
+    gram_matrix = all_sum(partial_value) / (levels * slots * degrees)
     return (spectral.reshape(vectors, levels, per_dev, 2, degrees), gram_matrix)
 
 
@@ -385,6 +428,9 @@
         and legendre.shape[0] * 2 % SUB == 0
         and vectors % CORES == 0
         and lon_dev % LANES == 0
+        and wave_of_slot.shape[0] * lon_dev * lax.axis_size("x") * CORES < 2**23
+        and lax.axis_size("x") > 1
+        and all(lax.axis_size(a) & (lax.axis_size(a) - 1) == 0 for a in ("lat", "x", "core"))
     )
     body = fast if fits else plain
     return body(grid_fields, legendre, wave_of_slot, energy_weight)

time: 646 us -> 577 us (0.89)
  blocking collectives: 44.8 us -> 0 us
  waiting for transfers between devices: 242 us -> 272 us
  local copies, waits for them, and re-layouts: 79.7 us -> 55.2 us
  Pallas kernels: 185 us -> 171 us
  starting transfers between devices: 72.3 us -> 59.3 us
    all_gather x1 -> x0, blocking collectives: 44.8 us -> none  [fast(): parts = lax.all_gather(partial_value, ('lat', 'x', 'core'))]
    pallas_call x8 -> x4, Pallas kernels: 95.1 us -> 59.9 us  [legendre_sums(): pl.pallas_call(functools.partial(legendre_kernel, bands, chunks, lat_dev,...]
    pallas_call x16 -> x14, Pallas kernels: 80.7 us -> 98.6 us  [fourier(): pl.pallas_call(functools.partial(fourier_kernel, scale, rows, add is not...]
    all_to_all x8 -> x7, starting transfers between devices: 57.7 us -> 40.2 us  [fast(): cofs.append(lax.all_to_all(mine, ('lat', 'core'), 0, 0, tiled=True))]
    ppermute x8 -> x7, waiting for transfers between devices: 242 us -> 259 us  [fast(): part = lax.ppermute(there, 'x', [(j, (j + step) % xs) for j in range(xs)])]
    another operation x8 -> x7, local copies, waits for them, and re-layouts: 21.4 us -> 7.35 us  [fast(): spectral = jnp.concatenate([d.reshape(shape) for d in done], axis=1)]
    ppermute x8 -> x12, starting transfers between devices: 1.73 us -> 8.98 us  [the longest x5 7.84 us: all_sum(): lax.ppermute(value, axis, [(i, i ^ step) for i in range(size)])]
    dynamic_slice x3 -> x4, local copies, waits for them, and re-layouts: 23.5 us -> 16.4 us  [fast(): away = lax.dynamic_slice_in_dim(by_field, away, rows.fields, 0)]
  transfers between devices with their start and end apart: 24 -> 26, of which waited for: 8 -> 12; matrix products, arithmetic and copies ran while one was open for 8% -> 7% of each run, Pallas kernels for 26% -> 24%
where the time goes in v2:
time: 577 us; the launch traced here: 567 us
  waiting for transfers between devices  272 us (47%)
  Pallas kernels  171 us (30%)
  starting transfers between devices  59.3 us (10%)
  local copies, waits for them, and re-layouts  55.2 us (10%)
  other arithmetic  8.07 us (1%)
    ppermute x7, waiting for transfers between devices, fast(): part = lax.ppermute(there, 'x', [(j, (j + step) % xs) for j in range(xs)])  259 us
    pallas_call x14, Pallas kernels, fourier(): pl.pallas_call(functools.partial(fourier_kernel, scale, rows, add is not...  98.6 us
    pallas_call x4, Pallas kernels, legendre_sums(): pl.pallas_call(functools.partial(legendre_kernel, bands, chunks, lat_dev,...  59.9 us
    all_to_all x7, starting transfers between devices, fast(): cofs.append(lax.all_to_all(mine, ('lat', 'core'), 0, 0, tiled=True))  40.2 us
    unnamed x48, local copies, waits for them, and re-layouts  25.6 us
    dynamic_slice x4, local copies, waits for them, and re-layouts, fast(): away = lax.dynamic_slice_in_dim(by_field, away, rows.fields, 0)  16.4 us
    pallas_call x1, Pallas kernels, gram_sums(): pl.pallas_call(functools.partial(gram_kernel, len(specs)), grid=(levels,...  12.6 us
  transfers between devices with their start and end apart: 26, of which 12 were waited for; matrix products, arithmetic and copies ran while one was open for 7% of the time, Pallas kernels for 24%

profile of v2, /device:TPU:0, one launch (start us, length us, event | category | flops | bytes accessed | tf_op | source)
XLA Modules:
  0.0 567.0 jit_solution(11218441507090135018)
XLA Ops:
  23.0 7.5 %fourier.16 = bf16[512,1920]{1,0:T(8,128)(2,1)} custom-call(s32[1]{0:T(128)} %bitcast.8.first, bf16[150,160,640]{2,1,0:T(8,128)(2,1)} %bitcast.35, bf16[150,160,640]{2,1,0:T(8,128)(2,1)} %bitcast.36, bf16[150,160,640]{2,1,0:T(8,128)(2,1)} %bitcast.37, bf16[150,160,640]{2,1,0:T(8,128)(2,1)} %bitcast.38, bf16[512,640]{1,0:T(8,128)(2,1)} %get-tuple-element.49.refs_3_.refs_4_, ...), custom_call_target="tpu_custom_call" | custom-call | flops 2516582400 | bytes 10158080 | tf_op jit(solution)/shard_map/fourier/pallas_call | solution.py:133
  37.3 50.6 %collective-permute-done.1.refs_6_ = bf16[512,512]{1,0:T(8,128)(2,1)S(1)} collective-permute-done((bf16[512,512]{1,0:T(8,128)(2,1)S(1)}, bf16[512,512]{1,0:T(8,128)(2,1)S(1)}, u32[]{:S(2)}, u32[]{:S(2)}) %collective-permute-start.1) | collective-permute-done | bytes 524320 | tf_op jit(solution)/shard_map/ppermute | solution.py:387
  98.6 7.8 %fourier.17 = bf16[512,1920]{1,0:T(8,128)(2,1)} custom-call(s32[1]{0:T(128)} %bitcast.8.first, bf16[150,160,640]{2,1,0:T(8,128)(2,1)} %bitcast.42, bf16[150,160,640]{2,1,0:T(8,128)(2,1)} %bitcast.43, bf16[150,160,640]{2,1,0:T(8,128)(2,1)} %bitcast.44, bf16[150,160,640]{2,1,0:T(8,128)(2,1)} %bitcast.45, bf16[512,640]{1,0:T(8,128)(2,1)} %get-tuple-element.47.refs_3_.refs_4_, ...), custom_call_target="tpu_custom_call" | custom-call | flops 2516582400 | bytes 10158080 | tf_op jit(solution)/shard_map/fourier/pallas_call | solution.py:133
  106.5 6.4 %all-to-all-done.refs_0_ = bf16[16,32,512]{2,1,0:T(8,128)(2,1)S(1)} async-done(((bf16[16,32,512]{2,1,0:T(8,128)(2,1)}), bf16[16,32,512]{2,1,0:T(8,128)(2,1)S(1)}, u32[]{:S(2)}, u32[]{:S(2)}) %all-to-all-start) | async-done | bytes 524320 | tf_op jit(solution)/shard_map/all_to_all | solution.py:397
  119.6 7.4 %fourier.18 = bf16[512,1920]{1,0:T(8,128)(2,1)} custom-call(s32[1]{0:T(128)} %bitcast.11.first, bf16[150,160,640]{2,1,0:T(8,128)(2,1)} %bitcast.46, bf16[150,160,640]{2,1,0:T(8,128)(2,1)} %bitcast.47, bf16[150,160,640]{2,1,0:T(8,128)(2,1)} %bitcast.48, bf16[150,160,640]{2,1,0:T(8,128)(2,1)} %bitcast.49, bf16[512,640]{1,0:T(8,128)(2,1)} %get-tuple-element.49.refs_3_.refs_4_, ...), custom_call_target="tpu_custom_call" | custom-call | flops 2516582400 | bytes 10158080 | tf_op jit(solution)/shard_map/fourier/pallas_call | solution.py:133
  133.6 38.7 %collective-permute-done.5.refs_7_ = bf16[512,1920]{1,0:T(8,128)(2,1)} collective-permute-done((bf16[512,1920]{1,0:T(8,128)(2,1)}, bf16[512,1920]{1,0:T(8,128)(2,1)}, u32[]{:S(2)}, u32[]{:S(2)}) %collective-permute-start.5) | collective-permute-done | bytes 1966112 | tf_op jit(solution)/shard_map/ppermute | solution.py:387
  172.3 7.8 %fourier.19 = bf16[512,1920]{1,0:T(8,128)(2,1)} custom-call(s32[1]{0:T(128)} %bitcast.11.first, bf16[150,160,640]{2,1,0:T(8,128)(2,1)} %bitcast.51, bf16[150,160,640]{2,1,0:T(8,128)(2,1)} %bitcast.52, bf16[150,160,640]{2,1,0:T(8,128)(2,1)} %bitcast.53, bf16[150,160,640]{2,1,0:T(8,128)(2,1)} %bitcast.54, bf16[512,640]{1,0:T(8,128)(2,1)} %get-tuple-element.47.refs_3_.refs_4_, ...), custom_call_target="tpu_custom_call" | custom-call | flops 2516582400 | bytes 10158080 | tf_op jit(solution)/shard_map/fourier/pallas_call | solution.py:133
  187.9 7.4 %fourier.20 = bf16[512,1920]{1,0:T(8,128)(2,1)} custom-call(s32[1]{0:T(128)} %bitcast.13.first, bf16[150,160,640]{2,1,0:T(8,128)(2,1)} %bitcast.58, bf16[150,160,640]{2,1,0:T(8,128)(2,1)} %bitcast.56, bf16[150,160,640]{2,1,0:T(8,128)(2,1)} %bitcast.57, bf16[150,160,640]{2,1,0:T(8,128)(2,1)} %bitcast.55, bf16[512,640]{1,0:T(8,128)(2,1)} %get-tuple-element.49.refs_3_.refs_4_, ...), custom_call_target="tpu_custom_call" | custom-call | flops 2516582400 | bytes 10158080 | tf_op jit(solution)/shard_map/fourier/pallas_call | solution.py:133
  197.0 43.7 %collective-permute-done.7.refs_7_ = bf16[512,1920]{1,0:T(8,128)(2,1)S(1)} collective-permute-done((bf16[512,1920]{1,0:T(8,128)(2,1)}, bf16[512,1920]{1,0:T(8,128)(2,1)S(1)}, u32[]{:S(2)}, u32[]{:S(2)}) %collective-permute-start.7) | collective-permute-done | bytes 1966112 | tf_op jit(solution)/shard_map/ppermute | solution.py:387
  242.0 7.9 %fourier.21 = bf16[512,1920]{1,0:T(8,128)(2,1)} custom-call(s32[1]{0:T(128)} %bitcast.13.first, bf16[150,160,640]{2,1,0:T(8,128)(2,1)} %bitcast.59, bf16[150,160,640]{2,1,0:T(8,128)(2,1)} %bitcast.60, bf16[150,160,640]{2,1,0:T(8,128)(2,1)} %bitcast.61, bf16[150,160,640]{2,1,0:T(8,128)(2,1)} %bitcast.62, bf16[512,640]{1,0:T(8,128)(2,1)} %get-tuple-element.47.refs_3_.refs_4_, ...), custom_call_target="tpu_custom_call" | custom-call | flops 2516582400 | bytes 10158080 | tf_op jit(solution)/shard_map/fourier/pallas_call | solution.py:133
  257.1 7.4 %fourier.22 = bf16[512,1920]{1,0:T(8,128)(2,1)} custom-call(s32[1]{0:T(128)} %bitcast.15.first, bf16[150,160,640]{2,1,0:T(8,128)(2,1)} %bitcast.63, bf16[150,160,640]{2,1,0:T(8,128)(2,1)} %bitcast.64, bf16[150,160,640]{2,1,0:T(8,128)(2,1)} %bitcast.65, bf16[150,160,640]{2,1,0:T(8,128)(2,1)} %bitcast.66, bf16[512,640]{1,0:T(8,128)(2,1)} %get-tuple-element.49.refs_3_.refs_4_, ...), custom_call_target="tpu_custom_call" | custom-call | flops 2516582400 | bytes 10158080 | tf_op jit(solution)/shard_map/fourier/pallas_call | solution.py:133
  271.2 38.8 %collective-permute-done.9.refs_7_ = bf16[512,1920]{1,0:T(8,128)(2,1)} collective-permute-done((bf16[512,1920]{1,0:T(8,128)(2,1)}, bf16[512,1920]{1,0:T(8,128)(2,1)}, u32[]{:S(2)}, u32[]{:S(2)}) %collective-permute-start.9) | collective-permute-done | bytes 1966112 | tf_op jit(solution)/shard_map/ppermute | solution.py:387
  309.9 7.8 %fourier.23 = bf16[512,1920]{1,0:T(8,128)(2,1)} custom-call(s32[1]{0:T(128)} %bitcast.15.first, bf16[150,160,640]{2,1,0:T(8,128)(2,1)} %bitcast.68, bf16[150,160,640]{2,1,0:T(8,128)(2,1)} %bitcast.69, bf16[150,160,640]{2,1,0:T(8,128)(2,1)} %bitcast.70, bf16[150,160,640]{2,1,0:T(8,128)(2,1)} %bitcast.71, bf16[512,640]{1,0:T(8,128)(2,1)} %get-tuple-element.47.refs_3_.refs_4_, ...), custom_call_target="tpu_custom_call" | custom-call | flops 2516582400 | bytes 10158080 | tf_op jit(solution)/shard_map/fourier/pallas_call | solution.py:133
  324.9 7.4 %fourier.24 = bf16[512,1920]{1,0:T(8,128)(2,1)} custom-call(s32[1]{0:T(128)} %bitcast.17.first, bf16[150,160,640]{2,1,0:T(8,128)(2,1)} %bitcast.72, bf16[150,160,640]{2,1,0:T(8,128)(2,1)} %bitcast.73, bf16[150,160,640]{2,1,0:T(8,128)(2,1)} %bitcast.74, bf16[150,160,640]{2,1,0:T(8,128)(2,1)} %bitcast.75, bf16[512,640]{1,0:T(8,128)(2,1)} %get-tuple-element.49.refs_3_.refs_4_, ...), custom_call_target="tpu_custom_call" | custom-call | flops 2516582400 | bytes 10158080 | tf_op jit(solution)/shard_map/fourier/pallas_call | solution.py:133
  333.9 43.7 %collective-permute-done.11.refs_7_ = bf16[512,1920]{1,0:T(8,128)(2,1)S(1)} collective-permute-done((bf16[512,1920]{1,0:T(8,128)(2,1)}, bf16[512,1920]{1,0:T(8,128)(2,1)S(1)}, u32[]{:S(2)}, u32[]{:S(2)}) %collective-permute-start.11) | collective-permute-done | bytes 1966112 | tf_op jit(solution)/shard_map/ppermute | solution.py:387
  378.9 7.8 %fourier.25 = bf16[512,1920]{1,0:T(8,128)(2,1)} custom-call(s32[1]{0:T(128)} %bitcast.17.first, bf16[150,160,640]{2,1,0:T(8,128)(2,1)} %bitcast.76, bf16[150,160,640]{2,1,0:T(8,128)(2,1)} %bitcast.77, bf16[150,160,640]{2,1,0:T(8,128)(2,1)} %bitcast.78, bf16[150,160,640]{2,1,0:T(8,128)(2,1)} %bitcast.79, bf16[512,640]{1,0:T(8,128)(2,1)} %get-tuple-element.47.refs_3_.refs_4_, ...), custom_call_target="tpu_custom_call" | custom-call | flops 2516582400 | bytes 10158080 | tf_op jit(solution)/shard_map/fourier/pallas_call | solution.py:133
  394.0 7.4 %fourier.26 = bf16[512,1920]{1,0:T(8,128)(2,1)} custom-call(s32[1]{0:T(128)} %bitcast.19.first, bf16[150,160,640]{2,1,0:T(8,128)(2,1)} %bitcast.80, bf16[150,160,640]{2,1,0:T(8,128)(2,1)} %bitcast.81, bf16[150,160,640]{2,1,0:T(8,128)(2,1)} %bitcast.82, bf16[150,160,640]{2,1,0:T(8,128)(2,1)} %bitcast.83, bf16[512,640]{1,0:T(8,128)(2,1)} %get-tuple-element.49.refs_3_.refs_4_, ...), custom_call_target="tpu_custom_call" | custom-call | flops 2516582400 | bytes 10158080 | tf_op jit(solution)/shard_map/fourier/pallas_call | solution.py:133
  402.8 43.8 %collective-permute-done.13.refs_7_ = bf16[512,1920]{1,0:T(8,128)(2,1)S(1)} collective-permute-done((bf16[512,1920]{1,0:T(8,128)(2,1)}, bf16[512,1920]{1,0:T(8,128)(2,1)S(1)}, u32[]{:S(2)}, u32[]{:S(2)}) %collective-permute-start.13) | collective-permute-done | bytes 1966112 | tf_op jit(solution)/shard_map/ppermute | solution.py:387
  447.9 7.8 %fourier.27 = bf16[512,1920]{1,0:T(8,128)(2,1)} custom-call(s32[1]{0:T(128)} %bitcast.19.first, bf16[150,160,640]{2,1,0:T(8,128)(2,1)} %bitcast.84, bf16[150,160,640]{2,1,0:T(8,128)(2,1)} %bitcast.85, bf16[150,160,640]{2,1,0:T(8,128)(2,1)} %bitcast.86, bf16[150,160,640]{2,1,0:T(8,128)(2,1)} %bitcast.87, bf16[512,640]{1,0:T(8,128)(2,1)} %get-tuple-element.47.refs_3_.refs_4_, ...), custom_call_target="tpu_custom_call" | custom-call | flops 2516582400 | bytes 10158080 | tf_op jit(solution)/shard_map/fourier/pallas_call | solution.py:133
  464.0 13.6 %legendre.4 = (bf16[6,32,640]{2,1,0:T(8,128)(2,1)}, bf16[24,32,640]{2,1,0:T(8,128)(2,1)}) custom-call(bf16[16,32,512]{2,1,0:T(8,128)(2,1)} %copy-done.12, bf16[16,32,1920]{2,1,0:T(8,128)(2,1)} %all-to-all-done.1.refs_1_, bf16[16,1280,640]{2,1,0:T(8,128)(2,1)} %refs_1_.1, s32[32,128]{1,0:T(8,128)} %broadcast_in_dim.20.refs_3_.refs_2_.refs_8_), custom_call_target="tpu_custom_call" | custom-call | flops 3145728000 | bytes 28704768 | tf_op jit(solution)/shard_map/legendre/pallas_call | solution.py:217
  483.6 16.9 %legendre.5 = (bf16[24,32,640]{2,1,0:T(8,128)(2,1)}, bf16[24,32,640]{2,1,0:T(8,128)(2,1)}) custom-call(bf16[16,32,1920]{2,1,0:T(8,128)(2,1)} %all-to-all-done.2.refs_0_, bf16[16,32,1920]{2,1,0:T(8,128)(2,1)} %all-to-all-done.3.refs_1_, bf16[16,1280,640]{2,1,0:T(8,128)(2,1)} %refs_1_.1, s32[32,128]{1,0:T(8,128)} %broadcast_in_dim.20.refs_3_.refs_2_.refs_8_), custom_call_target="tpu_custom_call" | custom-call | flops 5033164800 | bytes 30146560 | tf_op jit(solution)/shard_map/legendre/pallas_call | solution.py:217
  502.9 17.0 %legendre.6 = (bf16[24,32,640]{2,1,0:T(8,128)(2,1)}, bf16[24,32,640]{2,1,0:T(8,128)(2,1)}) custom-call(bf16[16,32,1920]{2,1,0:T(8,128)(2,1)} %all-to-all-done.4.refs_0_, bf16[16,32,1920]{2,1,0:T(8,128)(2,1)} %all-to-all-done.5.refs_1_, bf16[16,1280,640]{2,1,0:T(8,128)(2,1)} %refs_1_.1, s32[32,128]{1,0:T(8,128)} %broadcast_in_dim.20.refs_3_.refs_2_.refs_8_), custom_call_target="tpu_custom_call" | custom-call | flops 5033164800 | bytes 30146560 | tf_op jit(solution)/shard_map/legendre/pallas_call | solution.py:217
  521.2 12.4 %legendre.7 = bf16[24,32,640]{2,1,0:T(8,128)(2,1)} custom-call(bf16[16,32,1920]{2,1,0:T(8,128)(2,1)} %copy-done.7, bf16[16,1280,640]{2,1,0:T(8,128)(2,1)} %refs_1_.1, s32[32,128]{1,0:T(8,128)} %broadcast_in_dim.20.refs_3_.refs_2_.refs_8_), custom_call_target="tpu_custom_call" | custom-call | flops 2516582400 | bytes 28180480 | tf_op jit(solution)/shard_map/legendre/pallas_call | solution.py:217
  534.2 12.6 %gram.1 = f32[50,50]{1,0:T(8,128)} custom-call(bf16[2,3,32,640]{3,2,1,0:T(8,128)(2,1)} %bitcast.101, bf16[8,3,32,640]{3,2,1,0:T(8,128)(2,1)} %bitcast.97, bf16[8,3,32,640]{3,2,1,0:T(8,128)(2,1)} %bitcast.99, bf16[8,3,32,640]{3,2,1,0:T(8,128)(2,1)} %bitcast.98, bf16[8,3,32,640]{3,2,1,0:T(8,128)(2,1)} %bitcast.96, bf16[8,3,32,640]{3,2,1,0:T(8,128)(2,1)} %bitcast.95, ...), custom_call_target="tpu_custom_call" | custom-call | tf_op jit(solution)/shard_map/gram/pallas_call | solution.py:283
  (134 shorter events, 136.1 us)
Async XLA Ops:
  1.8 5.4 collective-permute-start
  16.7 4.9 collective-permute-start.2
  30.5 68.1 %collective-permute-start.3 = (bf16[512,1920]{1,0:T(8,128)(2,1)}, bf16[512,1920]{1,0:T(8,128)(2,1)}, u32[]{:S(2)}, u32[]{:S(2)}) collective-permute-start(bf16[512,1920]{1,0:T(8,128)(2,1)} %fourier.16), channel_id=1, source_target_pairs={{0,2},{2,0},{1,3},{3,1},{4,6},{6,4},{5,7},{7,5},{8,10},{10,8},{9,1... | collective-permute-start | bytes 5898248 | tf_op jit(solution)/shard_map/ppermute | solution.py:387
  33.1 54.8 %collective-permute-start.1 = (bf16[512,512]{1,0:T(8,128)(2,1)S(1)}, bf16[512,512]{1,0:T(8,128)(2,1)S(1)}, u32[]{:S(2)}, u32[]{:S(2)}) collective-permute-start(bf16[512,512]{1,0:T(8,128)(2,1)S(1)} %copy-done.16), channel_id=1, source_target_pairs={{0,2},{2,0},{1,3},{3,1},{4,6},{6,4},{5,7},{7,5},{8,10},{10,8},{9,1... | collective-permute-start | bytes 1572872 | tf_op jit(solution)/shard_map/ppermute | solution.py:387
  33.4 84.7 %collective-permute-start.4 = (bf16[12,160,640]{2,1,0:T(8,128)(2,1)}, bf16[12,160,640]{2,1,0:T(8,128)(2,1)S(1)}, u32[]{:S(2)}, u32[]{:S(2)}) collective-permute-start(bf16[12,160,640]{2,1,0:T(8,128)(2,1)} %get-tuple-element.44), channel_id=1, source_target_pairs={{0,1},{1,0},{2,3},{3,2},{4,5},{5,4},{6,7},{7,6},{8,9},{9,8},{10,11... | collective-permute-start | bytes 7372808 | tf_op jit(solution)/shard_map/ppermute | solution.py:383
  92.4 20.5 %all-to-all-start = ((bf16[16,32,512]{2,1,0:T(8,128)(2,1)}), bf16[16,32,512]{2,1,0:T(8,128)(2,1)S(1)}, u32[]{:S(2)}, u32[]{:S(2)}) async-start(bf16[16,32,512]{2,1,0:T(8,128)(2,1)} %bitcast.100), calls=%async_computation | async-start | bytes 1048576 | tf_op jit(solution)/shard_map/all_to_all | solution.py:397
  113.7 66.4 %all-to-all-start.1 = ((bf16[16,32,1920]{2,1,0:T(8,128)(2,1)}), bf16[16,32,1920]{2,1,0:T(8,128)(2,1)}, u32[]{:S(2)}, u32[]{:S(2)}) async-start(bf16[16,32,1920]{2,1,0:T(8,128)(2,1)} %bitcast.91), calls=%async_computation.1 | async-start | bytes 3932160 | tf_op jit(solution)/shard_map/all_to_all | solution.py:397
  127.0 45.3 %collective-permute-start.5 = (bf16[512,1920]{1,0:T(8,128)(2,1)}, bf16[512,1920]{1,0:T(8,128)(2,1)}, u32[]{:S(2)}, u32[]{:S(2)}) collective-permute-start(bf16[512,1920]{1,0:T(8,128)(2,1)} %fourier.18), channel_id=1, source_target_pairs={{0,2},{2,0},{1,3},{3,1},{4,6},{6,4},{5,7},{7,5},{8,10},{10,8},{9,1... | collective-permute-start | bytes 5898248 | tf_op jit(solution)/shard_map/ppermute | solution.py:387
  133.6 52.9 %collective-permute-start.6 = (bf16[12,160,640]{2,1,0:T(8,128)(2,1)}, bf16[12,160,640]{2,1,0:T(8,128)(2,1)S(1)}, u32[]{:S(2)}, u32[]{:S(2)}) collective-permute-start(bf16[12,160,640]{2,1,0:T(8,128)(2,1)} %get-tuple-element.43), channel_id=1, source_target_pairs={{0,1},{1,0},{2,3},{3,2},{4,5},{5,4},{6,7},{7,6},{8,9},{9,8},{10,11... | collective-permute-start | bytes 7372808 | tf_op jit(solution)/shard_map/ppermute | solution.py:383
  180.1 69.8 %all-to-all-start.2 = ((bf16[16,32,1920]{2,1,0:T(8,128)(2,1)}), bf16[16,32,1920]{2,1,0:T(8,128)(2,1)}, u32[]{:S(2)}, u32[]{:S(2)}) async-start(bf16[16,32,1920]{2,1,0:T(8,128)(2,1)} %bitcast.93), calls=%async_computation.2 | async-start | bytes 3932160 | tf_op jit(solution)/shard_map/all_to_all | solution.py:397
  195.3 45.4 %collective-permute-start.7 = (bf16[512,1920]{1,0:T(8,128)(2,1)}, bf16[512,1920]{1,0:T(8,128)(2,1)S(1)}, u32[]{:S(2)}, u32[]{:S(2)}) collective-permute-start(bf16[512,1920]{1,0:T(8,128)(2,1)} %fourier.20), channel_id=1, source_target_pairs={{0,2},{2,0},{1,3},{3,1},{4,6},{6,4},{5,7},{7,5},{8,10},{10,8},{9,1... | collective-permute-start | bytes 5898248 | tf_op jit(solution)/shard_map/ppermute | solution.py:387
  196.8 58.9 %collective-permute-start.8 = (bf16[12,160,640]{2,1,0:T(8,128)(2,1)}, bf16[12,160,640]{2,1,0:T(8,128)(2,1)S(1)}, u32[]{:S(2)}, u32[]{:S(2)}) collective-permute-start(bf16[12,160,640]{2,1,0:T(8,128)(2,1)} %get-tuple-element.42), channel_id=1, source_target_pairs={{0,1},{1,0},{2,3},{3,2},{4,5},{5,4},{6,7},{7,6},{8,9},{9,8},{10,11... | collective-permute-start | bytes 7372808 | tf_op jit(solution)/shard_map/ppermute | solution.py:383
  249.9 67.8 %all-to-all-start.3 = ((bf16[16,32,1920]{2,1,0:T(8,128)(2,1)}), bf16[16,32,1920]{2,1,0:T(8,128)(2,1)}, u32[]{:S(2)}, u32[]{:S(2)}) async-start(bf16[16,32,1920]{2,1,0:T(8,128)(2,1)} %bitcast.90), calls=%async_computation.3 | async-start | bytes 3932160 | tf_op jit(solution)/shard_map/all_to_all | solution.py:397
  264.5 45.4 %collective-permute-start.9 = (bf16[512,1920]{1,0:T(8,128)(2,1)}, bf16[512,1920]{1,0:T(8,128)(2,1)}, u32[]{:S(2)}, u32[]{:S(2)}) collective-permute-start(bf16[512,1920]{1,0:T(8,128)(2,1)} %fourier.22), channel_id=1, source_target_pairs={{0,2},{2,0},{1,3},{3,1},{4,6},{6,4},{5,7},{7,5},{8,10},{10,8},{9,1... | collective-permute-start | bytes 5898248 | tf_op jit(solution)/shard_map/ppermute | solution.py:387
  271.1 52.4 %collective-permute-start.10 = (bf16[12,160,640]{2,1,0:T(8,128)(2,1)}, bf16[12,160,640]{2,1,0:T(8,128)(2,1)S(1)}, u32[]{:S(2)}, u32[]{:S(2)}) collective-permute-start(bf16[12,160,640]{2,1,0:T(8,128)(2,1)} %get-tuple-element.41), channel_id=1, source_target_pairs={{0,1},{1,0},{2,3},{3,2},{4,5},{5,4},{6,7},{7,6},{8,9},{9,8},{10,11... | collective-permute-start | bytes 7372808 | tf_op jit(solution)/shard_map/ppermute | solution.py:383
  317.7 69.0 %all-to-all-start.4 = ((bf16[16,32,1920]{2,1,0:T(8,128)(2,1)}), bf16[16,32,1920]{2,1,0:T(8,128)(2,1)}, u32[]{:S(2)}, u32[]{:S(2)}) async-start(bf16[16,32,1920]{2,1,0:T(8,128)(2,1)} %bitcast.94), calls=%async_computation.4 | async-start | bytes 3932160 | tf_op jit(solution)/shard_map/all_to_all | solution.py:397
  332.3 45.3 %collective-permute-start.11 = (bf16[512,1920]{1,0:T(8,128)(2,1)}, bf16[512,1920]{1,0:T(8,128)(2,1)S(1)}, u32[]{:S(2)}, u32[]{:S(2)}) collective-permute-start(bf16[512,1920]{1,0:T(8,128)(2,1)} %fourier.24), channel_id=1, source_target_pairs={{0,2},{2,0},{1,3},{3,1},{4,6},{6,4},{5,7},{7,5},{8,10},{10,8},{9,1... | collective-permute-start | bytes 5898248 | tf_op jit(solution)/shard_map/ppermute | solution.py:387
  333.8 58.7 %collective-permute-start.12 = (bf16[12,160,640]{2,1,0:T(8,128)(2,1)}, bf16[12,160,640]{2,1,0:T(8,128)(2,1)S(1)}, u32[]{:S(2)}, u32[]{:S(2)}) collective-permute-start(bf16[12,160,640]{2,1,0:T(8,128)(2,1)} %get-tuple-element.40), channel_id=1, source_target_pairs={{0,1},{1,0},{2,3},{3,2},{4,5},{5,4},{6,7},{7,6},{8,9},{9,8},{10,11... | collective-permute-start | bytes 7372808 | tf_op jit(solution)/shard_map/ppermute | solution.py:383
  386.7 69.0 %all-to-all-start.5 = ((bf16[16,32,1920]{2,1,0:T(8,128)(2,1)}), bf16[16,32,1920]{2,1,0:T(8,128)(2,1)}, u32[]{:S(2)}, u32[]{:S(2)}) async-start(bf16[16,32,1920]{2,1,0:T(8,128)(2,1)} %bitcast.92), calls=%async_computation.5 | async-start | bytes 3932160 | tf_op jit(solution)/shard_map/all_to_all | solution.py:397
  401.4 45.3 %collective-permute-start.13 = (bf16[512,1920]{1,0:T(8,128)(2,1)}, bf16[512,1920]{1,0:T(8,128)(2,1)S(1)}, u32[]{:S(2)}, u32[]{:S(2)}) collective-permute-start(bf16[512,1920]{1,0:T(8,128)(2,1)} %fourier.26), channel_id=1, source_target_pairs={{0,2},{2,0},{1,3},{3,1},{4,6},{6,4},{5,7},{7,5},{8,10},{10,8},{9,1... | collective-permute-start | bytes 5898248 | tf_op jit(solution)/shard_map/ppermute | solution.py:387
  455.7 64.2 %all-to-all-start.6 = ((bf16[16,32,1920]{2,1,0:T(8,128)(2,1)}), bf16[16,32,1920]{2,1,0:T(8,128)(2,1)S(1)}, u32[]{:S(2)}, u32[]{:S(2)}) async-start(bf16[16,32,1920]{2,1,0:T(8,128)(2,1)} %bitcast.89), calls=%async_computation.6 | async-start | bytes 3932160 | tf_op jit(solution)/shard_map/all_to_all | solution.py:397
  549.7 3.9 collective-permute-start.15
  553.6 3.9 collective-permute-start.16
  561.4 4.8 collective-permute-start.18
  (23 other events, 60.5 us)

commit v3 on v2

--- a/solution.py
+++ b/solution.py
@@ -234,15 +234,16 @@
     )(*cofs, leg, waves)
 
 
-def gram_kernel(groups, *refs):
+def gram_kernel(groups, rows, vectors, *refs):
     specs = refs[:groups]
-    weight, wave, place, out, total = refs[groups:]
+    weight, wave, place, before, out, total = refs[groups:]
     step = pl.program_id(0) * pl.num_programs(1) + pl.program_id(1)
     values = jnp.concatenate([r[...].reshape(-1, r.shape[-1]) for r in specs], axis=0)
-    rows, degrees = values.shape
-    vectors = rows // SUB
+    whole, degrees = values.shape
+    old = whole - rows
     factor = jnp.where(wave[:, :1] == 0, 1.0, 2.0).astype(jnp.float32)
-    scaled = values.astype(jnp.float32).reshape(vectors, SUB, degrees) * (factor * weight[0])[None]
+    scaled = values[old:].astype(jnp.float32).reshape(rows // SUB, SUB, degrees)
+    scaled = scaled * (factor * weight[0])[None]
     scaled = scaled.reshape(rows, degrees).astype(jnp.bfloat16)
     part = lax.dot_general(
         scaled, values, (((1,), (1,)), ((), ())), preferred_element_type=jnp.float32
@@ -256,32 +257,36 @@
     def _():
         total[...] += part
 
+    def mul(x, y):
+        dims = (((1,), (1,)), ((), ()))
+        return lax.dot_general(
+            x, y, dims, preferred_element_type=jnp.float32, precision=lax.Precision.HIGHEST
+        )
+
     @pl.when(step == pl.num_programs(0) * pl.num_programs(1) - 1)
     def _():
-        row = lax.broadcasted_iota(jnp.int32, (rows, rows), 0)
-        col = lax.broadcasted_iota(jnp.int32, (rows, rows), 1)
+        row = lax.broadcasted_iota(jnp.int32, (rows, whole), 0)
+        col = lax.broadcasted_iota(jnp.int32, (rows, whole), 1)
         kept = jnp.where(row % SUB == col % SUB, total[...], 0.0)
-        slot = lax.broadcasted_iota(jnp.int32, (vectors, rows), 0)
+        slot = lax.broadcasted_iota(jnp.int32, (vectors, whole), 0)
         pick = (place[:1, :] == slot).astype(jnp.float32)
-        half = jnp.dot(
-            pick, kept, preferred_element_type=jnp.float32, precision=lax.Precision.HIGHEST
-        )
-        out[...] = lax.dot_general(
-            half,
-            pick,
-            (((1,), (1,)), ((), ())),
-            preferred_element_type=jnp.float32,
-            precision=lax.Precision.HIGHEST,
-        )
-
-
-def gram_sums(specs, order, weight, waves):
+        seen = lax.broadcasted_iota(jnp.int32, (vectors, whole), 1)
+        ours = jnp.where(seen < old, 0.0, pick)[:, old:] if old else pick
+        across = mul(pick, kept)
+        found = before[...] + mul(ours, across)
+        if old:
+            found += mul(mul(jnp.where(seen < old, pick, 0.0), kept), ours)
+        out[...] = found
+
+
+def gram_sums(specs, order, last, vectors, before, weight, waves):
     _, levels, slot_rows, degrees = specs[0].shape
-    vectors = len(order)
+    rows = len(order) * SUB
     place = jnp.repeat(jnp.asarray(order, jnp.int32), SUB)
-    place = jnp.broadcast_to(place[None], (SUB, vectors * SUB))
+    place = jnp.broadcast_to(place[None], (SUB, rows))
+    square = pl.BlockSpec((vectors, vectors), lambda l, i: (0, 0))
     return pl.pallas_call(
-        functools.partial(gram_kernel, len(specs)),
+        functools.partial(gram_kernel, len(specs), last * SUB, vectors),
         grid=(levels, slot_rows // SUB),
         in_specs=[
             pl.BlockSpec((s.shape[0], 1, SUB, degrees), lambda l, i: (0, l, i, 0)) for s in specs
@@ -289,19 +294,20 @@
         + [
             pl.BlockSpec((1, 1, degrees), lambda l, i: (l, 0, 0)),
             pl.BlockSpec((SUB, LANES), lambda l, i: (i, 0)),
-            pl.BlockSpec((SUB, vectors * SUB), lambda l, i: (0, 0)),
+            pl.BlockSpec((SUB, rows), lambda l, i: (0, 0)),
+            square,
         ],
-        out_specs=pl.BlockSpec((vectors, vectors), lambda l, i: (0, 0)),
+        out_specs=square,
         out_shape=jax.ShapeDtypeStruct((vectors, vectors), jnp.float32),
-        scratch_shapes=[pltpu.VMEM((vectors * SUB, vectors * SUB), jnp.float32)],
+        scratch_shapes=[pltpu.VMEM((last * SUB, rows), jnp.float32)],
         compiler_params=pltpu.CompilerParams(vmem_limit_bytes=VMEM),
         name="gram",
-    )(*specs, weight.reshape(levels, 1, degrees), waves, place)
+    )(*specs, weight.reshape(levels, 1, degrees), waves, place, before)
 
 
 def chunk_sizes(half, quad):
-    first = half % quad
-    return ([first] if first else []) + [quad] * (half // quad)
+    ramp = half % quad + quad
+    return [ramp // 2, ramp - ramp // 2] + [quad] * ((half - ramp) // quad)
 
 
 def groups_of(count):
@@ -411,7 +417,11 @@
     ]
     shape = (CORES, -1, levels, per_dev, 2, degrees)
     spectral = jnp.concatenate([d.reshape(shape) for d in done], axis=1)
-    partial_value = gram_sums(done, order, energy_weight, wave_rows)
+    tail = CORES * sizes[-1]
+    grams = functools.partial(gram_sums, vectors=vectors, weight=energy_weight, waves=wave_rows)
+    empty = jnp.zeros((vectors, vectors), jnp.float32)
+    partial_value = grams(done[:-1], order[:-tail], vectors - tail, before=empty)
+    partial_value = grams(done, order, tail, before=partial_value)
     gram_matrix = all_sum(partial_value) / (levels * slots * degrees)
     return (spectral.reshape(vectors, levels, per_dev, 2, degrees), gram_matrix)
 

time: 577 us -> 585 us (1.014)
  Pallas kernels: 171 us -> 182 us
  waiting for transfers between devices: 272 us -> 265 us
    pallas_call x1 -> x2, Pallas kernels: 12.6 us -> 22.7 us  [gram_sums(): pl.pallas_call(functools.partial(gram_kernel, len(specs), last * SUB, vec...]
    all_to_all x7, waiting for transfers between devices: 6.44 us -> 0.02 us  [fast(): cofs.append(lax.all_to_all(mine, ('lat', 'core'), 0, 0, tiled=True))]
    dynamic_slice x4 -> x5, local copies, waits for them, and re-layouts: 16.4 us -> 17.9 us  [fast(): away = lax.dynamic_slice_in_dim(by_field, away, rows.fields, 0)]
    unnamed x48 -> x50, local copies, waits for them, and re-layouts: 25.6 us -> 24.8 us
  transfers between devices with their start and end apart: 26 -> 26, of which waited for: 12 -> 11; matrix products, arithmetic and copies ran while one was open for 7% -> 8% of each run, Pallas kernels for 24% -> 27%
where the time goes in v3:
time: 585 us; the launch traced here: 575 us
  waiting for transfers between devices  265 us (45%)
  Pallas kernels  182 us (31%)
  starting transfers between devices  62.7 us (11%)
  local copies, waits for them, and re-layouts  55.5 us (9%)
  other arithmetic  8.05 us (1%)
    ppermute x7, waiting for transfers between devices, fast(): part = lax.ppermute(there, 'x', [(j, (j + step) % xs) for j in range(xs)])  263 us
    pallas_call x14, Pallas kernels, fourier(): pl.pallas_call(functools.partial(fourier_kernel, scale, rows, add is not...  99.8 us
    pallas_call x4, Pallas kernels, legendre_sums(): pl.pallas_call(functools.partial(legendre_kernel, bands, chunks, lat_dev,...  59.8 us
    all_to_all x7, starting transfers between devices, fast(): cofs.append(lax.all_to_all(mine, ('lat', 'core'), 0, 0, tiled=True))  41.6 us
    unnamed x50, local copies, waits for them, and re-layouts  24.8 us
    pallas_call x2, Pallas kernels, gram_sums(): pl.pallas_call(functools.partial(gram_kernel, len(specs), last * SUB, vec...  22.7 us
    dynamic_slice x5, local copies, waits for them, and re-layouts, fast(): away = lax.dynamic_slice_in_dim(by_field, away, rows.fields, 0)  17.9 us
    ppermute x7, starting transfers between devices, fast(): part = lax.ppermute(there, 'x', [(j, (j + step) % xs) for j in range(xs)])  11.8 us
  transfers between devices with their start and end apart: 26, of which 11 were waited for; matrix products, arithmetic and copies ran while one was open for 8% of the time, Pallas kernels for 27%

profile of v3, /device:TPU:0, one launch (start us, length us, event | category | flops | bytes accessed | tf_op | source)
XLA Modules:
  0.0 575.1 jit_solution(5125939488126787717)
XLA Ops:
  22.8 19.6 %collective-permute-done.1.refs_9_ = bf16[512,1024]{1,0:T(8,128)(2,1)} collective-permute-done((bf16[512,1024]{1,0:T(8,128)(2,1)S(1)}, bf16[512,1024]{1,0:T(8,128)(2,1)}, u32[]{:S(2)}, u32[]{:S(2)}) %collective-permute-start.1) | collective-permute-done | bytes 1048608 | tf_op jit(solution)/shard_map/ppermute | solution.py:393
  66.7 35.2 %collective-permute-done.3.refs_12_ = bf16[512,1536]{1,0:T(8,128)(2,1)S(1)} collective-permute-done((bf16[512,1536]{1,0:T(8,128)(2,1)}, bf16[512,1536]{1,0:T(8,128)(2,1)S(1)}, u32[]{:S(2)}, u32[]{:S(2)}) %collective-permute-start.3) | collective-permute-done | bytes 1572896 | tf_op jit(solution)/shard_map/ppermute | solution.py:393
  103.1 6.9 %fourier.17 = bf16[512,1536]{1,0:T(8,128)(2,1)} custom-call(s32[1]{0:T(128)} %bitcast.8.first, bf16[150,160,640]{2,1,0:T(8,128)(2,1)} %bitcast.52, bf16[150,160,640]{2,1,0:T(8,128)(2,1)} %bitcast.53, bf16[150,160,640]{2,1,0:T(8,128)(2,1)} %bitcast.54, bf16[150,160,640]{2,1,0:T(8,128)(2,1)} %bitcast.55, bf16[150,160,640]{2,1,0:T(8,128)(2,1)} %bitcast.56, ...), custom_call_target="tpu_custom_call" | custom-call | flops 2013265920 | bytes 8388608 | tf_op jit(solution)/shard_map/fourier/pallas_call | solution.py:133
  116.2 7.4 %fourier.18 = bf16[512,1920]{1,0:T(8,128)(2,1)} custom-call(s32[1]{0:T(128)} %bitcast.10.first, bf16[150,160,640]{2,1,0:T(8,128)(2,1)} %bitcast.61, bf16[150,160,640]{2,1,0:T(8,128)(2,1)} %bitcast.62, bf16[150,160,640]{2,1,0:T(8,128)(2,1)} %bitcast.63, bf16[150,160,640]{2,1,0:T(8,128)(2,1)} %bitcast.64, ...), custom_call_target="tpu_custom_call" | custom-call | flops 2516582400 | bytes 10158080 | tf_op jit(solution)/shard_map/fourier/pallas_call | solution.py:133
  130.5 38.7 %collective-permute-done.5.refs_7_ = bf16[512,1920]{1,0:T(8,128)(2,1)} collective-permute-done((bf16[512,1920]{1,0:T(8,128)(2,1)}, bf16[512,1920]{1,0:T(8,128)(2,1)}, u32[]{:S(2)}, u32[]{:S(2)}) %collective-permute-start.5) | collective-permute-done | bytes 1966112 | tf_op jit(solution)/shard_map/ppermute | solution.py:393
  169.2 7.8 %fourier.19 = bf16[512,1920]{1,0:T(8,128)(2,1)} custom-call(s32[1]{0:T(128)} %bitcast.10.first, bf16[150,160,640]{2,1,0:T(8,128)(2,1)} %bitcast.66, bf16[150,160,640]{2,1,0:T(8,128)(2,1)} %bitcast.67, bf16[150,160,640]{2,1,0:T(8,128)(2,1)} %bitcast.68, bf16[150,160,640]{2,1,0:T(8,128)(2,1)} %bitcast.69, ...), custom_call_target="tpu_custom_call" | custom-call | flops 2516582400 | bytes 10158080 | tf_op jit(solution)/shard_map/fourier/pallas_call | solution.py:133
  184.2 7.4 %fourier.20 = bf16[512,1920]{1,0:T(8,128)(2,1)} custom-call(s32[1]{0:T(128)} %bitcast.12.first, bf16[150,160,640]{2,1,0:T(8,128)(2,1)} %bitcast.70, bf16[150,160,640]{2,1,0:T(8,128)(2,1)} %bitcast.71, bf16[150,160,640]{2,1,0:T(8,128)(2,1)} %bitcast.72, bf16[150,160,640]{2,1,0:T(8,128)(2,1)} %bitcast.73, ...), custom_call_target="tpu_custom_call" | custom-call | flops 2516582400 | bytes 10158080 | tf_op jit(solution)/shard_map/fourier/pallas_call | solution.py:133
  193.2 43.7 %collective-permute-done.7.refs_7_ = bf16[512,1920]{1,0:T(8,128)(2,1)S(1)} collective-permute-done((bf16[512,1920]{1,0:T(8,128)(2,1)}, bf16[512,1920]{1,0:T(8,128)(2,1)S(1)}, u32[]{:S(2)}, u32[]{:S(2)}) %collective-permute-start.7) | collective-permute-done | bytes 1966112 | tf_op jit(solution)/shard_map/ppermute | solution.py:393
  238.2 7.8 %fourier.21 = bf16[512,1920]{1,0:T(8,128)(2,1)} custom-call(s32[1]{0:T(128)} %bitcast.12.first, bf16[150,160,640]{2,1,0:T(8,128)(2,1)} %bitcast.74, bf16[150,160,640]{2,1,0:T(8,128)(2,1)} %bitcast.75, bf16[150,160,640]{2,1,0:T(8,128)(2,1)} %bitcast.76, bf16[150,160,640]{2,1,0:T(8,128)(2,1)} %bitcast.77, ...), custom_call_target="tpu_custom_call" | custom-call | flops 2516582400 | bytes 10158080 | tf_op jit(solution)/shard_map/fourier/pallas_call | solution.py:133
  253.2 7.4 %fourier.22 = bf16[512,1920]{1,0:T(8,128)(2,1)} custom-call(s32[1]{0:T(128)} %bitcast.14.first, bf16[150,160,640]{2,1,0:T(8,128)(2,1)} %bitcast.78, bf16[150,160,640]{2,1,0:T(8,128)(2,1)} %bitcast.79, bf16[150,160,640]{2,1,0:T(8,128)(2,1)} %bitcast.80, bf16[150,160,640]{2,1,0:T(8,128)(2,1)} %bitcast.81, ...), custom_call_target="tpu_custom_call" | custom-call | flops 2516582400 | bytes 10158080 | tf_op jit(solution)/shard_map/fourier/pallas_call | solution.py:133
  267.3 38.8 %collective-permute-done.9.refs_7_ = bf16[512,1920]{1,0:T(8,128)(2,1)} collective-permute-done((bf16[512,1920]{1,0:T(8,128)(2,1)}, bf16[512,1920]{1,0:T(8,128)(2,1)}, u32[]{:S(2)}, u32[]{:S(2)}) %collective-permute-start.9) | collective-permute-done | bytes 1966112 | tf_op jit(solution)/shard_map/ppermute | solution.py:393
  306.0 7.8 %fourier.23 = bf16[512,1920]{1,0:T(8,128)(2,1)} custom-call(s32[1]{0:T(128)} %bitcast.14.first, bf16[150,160,640]{2,1,0:T(8,128)(2,1)} %bitcast.83, bf16[150,160,640]{2,1,0:T(8,128)(2,1)} %bitcast.84, bf16[150,160,640]{2,1,0:T(8,128)(2,1)} %bitcast.85, bf16[150,160,640]{2,1,0:T(8,128)(2,1)} %bitcast.86, ...), custom_call_target="tpu_custom_call" | custom-call | flops 2516582400 | bytes 10158080 | tf_op jit(solution)/shard_map/fourier/pallas_call | solution.py:133
  321.1 7.5 %fourier.24 = bf16[512,1920]{1,0:T(8,128)(2,1)} custom-call(s32[1]{0:T(128)} %bitcast.16.first, bf16[150,160,640]{2,1,0:T(8,128)(2,1)} %bitcast.87, bf16[150,160,640]{2,1,0:T(8,128)(2,1)} %bitcast.88, bf16[150,160,640]{2,1,0:T(8,128)(2,1)} %bitcast.89, bf16[150,160,640]{2,1,0:T(8,128)(2,1)} %bitcast.90, ...), custom_call_target="tpu_custom_call" | custom-call | flops 2516582400 | bytes 10158080 | tf_op jit(solution)/shard_map/fourier/pallas_call | solution.py:133
  330.1 43.7 %collective-permute-done.11.refs_7_ = bf16[512,1920]{1,0:T(8,128)(2,1)S(1)} collective-permute-done((bf16[512,1920]{1,0:T(8,128)(2,1)}, bf16[512,1920]{1,0:T(8,128)(2,1)S(1)}, u32[]{:S(2)}, u32[]{:S(2)}) %collective-permute-start.11) | collective-permute-done | bytes 1966112 | tf_op jit(solution)/shard_map/ppermute | solution.py:393
  375.2 7.9 %fourier.25 = bf16[512,1920]{1,0:T(8,128)(2,1)} custom-call(s32[1]{0:T(128)} %bitcast.16.first, bf16[150,160,640]{2,1,0:T(8,128)(2,1)} %bitcast.91, bf16[150,160,640]{2,1,0:T(8,128)(2,1)} %bitcast.92, bf16[150,160,640]{2,1,0:T(8,128)(2,1)} %bitcast.93, bf16[150,160,640]{2,1,0:T(8,128)(2,1)} %bitcast.94, ...), custom_call_target="tpu_custom_call" | custom-call | flops 2516582400 | bytes 10158080 | tf_op jit(solution)/shard_map/fourier/pallas_call | solution.py:133
  390.3 7.4 %fourier.26 = bf16[512,1920]{1,0:T(8,128)(2,1)} custom-call(s32[1]{0:T(128)} %bitcast.18.first, bf16[150,160,640]{2,1,0:T(8,128)(2,1)} %bitcast.95, bf16[150,160,640]{2,1,0:T(8,128)(2,1)} %bitcast.96, bf16[150,160,640]{2,1,0:T(8,128)(2,1)} %bitcast.97, bf16[150,160,640]{2,1,0:T(8,128)(2,1)} %bitcast.98, ...), custom_call_target="tpu_custom_call" | custom-call | flops 2516582400 | bytes 10158080 | tf_op jit(solution)/shard_map/fourier/pallas_call | solution.py:133
  399.1 43.8 %collective-permute-done.13.refs_7_ = bf16[512,1920]{1,0:T(8,128)(2,1)S(1)} collective-permute-done((bf16[512,1920]{1,0:T(8,128)(2,1)}, bf16[512,1920]{1,0:T(8,128)(2,1)S(1)}, u32[]{:S(2)}, u32[]{:S(2)}) %collective-permute-start.13) | collective-permute-done | bytes 1966112 | tf_op jit(solution)/shard_map/ppermute | solution.py:393
  444.2 7.8 %fourier.27 = bf16[512,1920]{1,0:T(8,128)(2,1)} custom-call(s32[1]{0:T(128)} %bitcast.18.first, bf16[150,160,640]{2,1,0:T(8,128)(2,1)} %bitcast.99, bf16[150,160,640]{2,1,0:T(8,128)(2,1)} %bitcast.100, bf16[150,160,640]{2,1,0:T(8,128)(2,1)} %bitcast.101, bf16[150,160,640]{2,1,0:T(8,128)(2,1)} %bitcast.102, ...), custom_call_target="tpu_custom_call" | custom-call | flops 2516582400 | bytes 10158080 | tf_op jit(solution)/shard_map/fourier/pallas_call | solution.py:133
  460.7 13.5 %legendre.4 = (bf16[12,32,640]{2,1,0:T(8,128)(2,1)}, bf16[18,32,640]{2,1,0:T(8,128)(2,1)}) custom-call(bf16[16,32,1024]{2,1,0:T(8,128)(2,1)} %all-to-all-done.refs_0_, bf16[16,32,1536]{2,1,0:T(8,128)(2,1)} %all-to-all-done.1.refs_1_, bf16[16,1280,640]{2,1,0:T(8,128)(2,1)} %refs_1_.1, s32[32,128]{1,0:T(8,128)} %broadcast_in_dim.28.refs_3_.refs_2_.refs_7_.refs_8_), custom_call_target="tpu_custom_call" | custom-call | flops 3145728000 | bytes 28835840 | tf_op jit(solution)/shard_map/legendre/pallas_call | solution.py:217
  480.1 16.9 %legendre.5 = (bf16[24,32,640]{2,1,0:T(8,128)(2,1)}, bf16[24,32,640]{2,1,0:T(8,128)(2,1)}) custom-call(bf16[16,32,1920]{2,1,0:T(8,128)(2,1)} %all-to-all-done.2.refs_0_, bf16[16,32,1920]{2,1,0:T(8,128)(2,1)} %all-to-all-done.3.refs_1_, bf16[16,1280,640]{2,1,0:T(8,128)(2,1)} %refs_1_.1, s32[32,128]{1,0:T(8,128)} %broadcast_in_dim.28.refs_3_.refs_2_.refs_7_.refs_8_), custom_call_target="tpu_custom_call" | custom-call | flops 5033164800 | bytes 30146560 | tf_op jit(solution)/shard_map/legendre/pallas_call | solution.py:217
  499.5 17.0 %legendre.6 = (bf16[24,32,640]{2,1,0:T(8,128)(2,1)}, bf16[24,32,640]{2,1,0:T(8,128)(2,1)}) custom-call(bf16[16,32,1920]{2,1,0:T(8,128)(2,1)} %all-to-all-done.4.refs_0_, bf16[16,32,1920]{2,1,0:T(8,128)(2,1)} %all-to-all-done.5.refs_1_, bf16[16,1280,640]{2,1,0:T(8,128)(2,1)} %refs_1_.1, s32[32,128]{1,0:T(8,128)} %broadcast_in_dim.28.refs_3_.refs_2_.refs_7_.refs_8_), custom_call_target="tpu_custom_call" | custom-call | flops 5033164800 | bytes 30146560 | tf_op jit(solution)/shard_map/legendre/pallas_call | solution.py:217
  517.6 11.8 %gram.2.refs_10_ = f32[50,50]{1,0:T(8,128)} custom-call(bf16[4,3,32,640]{3,2,1,0:T(8,128)(2,1)} %bitcast.120, bf16[6,3,32,640]{3,2,1,0:T(8,128)(2,1)} %bitcast.117, bf16[8,3,32,640]{3,2,1,0:T(8,128)(2,1)} %bitcast.110, bf16[8,3,32,640]{3,2,1,0:T(8,128)(2,1)} %bitcast.108, bf16[8,3,32,640]{3,2,1,0:T(8,128)(2,1)} %bitcast.106, ...), custom_call_target="tpu_custom_call" | custom-call | tf_op jit(solution)/shard_map/gram/pallas_call | solution.py:288
  530.7 12.4 %legendre.7 = bf16[24,32,640]{2,1,0:T(8,128)(2,1)} custom-call(bf16[16,32,1920]{2,1,0:T(8,128)(2,1)} %copy-done.8, bf16[16,1280,640]{2,1,0:T(8,128)(2,1)} %refs_1_.1, s32[32,128]{1,0:T(8,128)} %broadcast_in_dim.28.refs_3_.refs_2_.refs_7_.refs_8_), custom_call_target="tpu_custom_call" | custom-call | flops 2516582400 | bytes 28180480 | tf_op jit(solution)/shard_map/legendre/pallas_call | solution.py:217
  543.7 10.9 %gram.3 = f32[50,50]{1,0:T(8,128)} custom-call(bf16[4,3,32,640]{3,2,1,0:T(8,128)(2,1)} %bitcast.121, bf16[6,3,32,640]{3,2,1,0:T(8,128)(2,1)} %bitcast.118, bf16[8,3,32,640]{3,2,1,0:T(8,128)(2,1)} %bitcast.111, bf16[8,3,32,640]{3,2,1,0:T(8,128)(2,1)} %bitcast.109, bf16[8,3,32,640]{3,2,1,0:T(8,128)(2,1)} %bitcast.107, bf16[8,3,32,640]{3,2,1,0:T(8,128)(2,1)} %bitcast.104, ...), custom_call_target="tpu_custom_call" | custom-call | tf_op jit(solution)/shard_map/gram/pallas_call | solution.py:288
  (142 shorter events, 144.6 us)
Async XLA Ops:
  2.0 4.7 collective-permute-start
  15.9 41.7 %collective-permute-start.2 = (bf16[9,160,640]{2,1,0:T(8,128)(2,1)}, bf16[9,160,640]{2,1,0:T(8,128)(2,1)S(1)}, u32[]{:S(2)}, u32[]{:S(2)}) collective-permute-start(bf16[9,160,640]{2,1,0:T(8,128)(2,1)} %constant_dynamic-slice_fusion.5), channel_id=1, source_target_pairs={{0,1},{1,0},{2,3},{3,2},{4,5},{5,4},{6,7},{7,6},{8,9},{9,8},{10,11... | collective-permute-start | bytes 5529608 | tf_op jit(solution)/shard_map/ppermute | solution.py:389
  15.9 26.4 %collective-permute-start.1 = (bf16[512,1024]{1,0:T(8,128)(2,1)S(1)}, bf16[512,1024]{1,0:T(8,128)(2,1)}, u32[]{:S(2)}, u32[]{:S(2)}) collective-permute-start(bf16[512,1024]{1,0:T(8,128)(2,1)S(1)} %copy-done.16), channel_id=1, source_target_pairs={{0,2},{2,0},{1,3},{3,1},{4,6},{6,4},{5,7},{7,5},{8,10},{10,8},{9,1... | collective-permute-start | bytes 3145736 | tf_op jit(solution)/shard_map/ppermute | solution.py:393
  47.6 62.4 %all-to-all-start = ((bf16[16,32,1024]{2,1,0:T(8,128)(2,1)}), bf16[16,32,1024]{2,1,0:T(8,128)(2,1)}, u32[]{:S(2)}, u32[]{:S(2)}) async-start(bf16[16,32,1024]{2,1,0:T(8,128)(2,1)} %bitcast.122), calls=%async_computation | async-start | bytes 2097152 | tf_op jit(solution)/shard_map/all_to_all | solution.py:403
  57.2 59.0 %collective-permute-start.4 = (bf16[12,160,640]{2,1,0:T(8,128)(2,1)}, bf16[12,160,640]{2,1,0:T(8,128)(2,1)}, u32[]{:S(2)}, u32[]{:S(2)}) collective-permute-start(bf16[12,160,640]{2,1,0:T(8,128)(2,1)} %constant_dynamic-slice_fusion.4), channel_id=1, source_target_pairs={{0,1},{1,0},{2,3},{3,2},{4,5},{5,4},{6,7},{7,6},{8,9},{9,8},{10,11... | collective-permute-start | bytes 7372808 | tf_op jit(solution)/shard_map/ppermute | solution.py:389
  65.2 36.7 %collective-permute-start.3 = (bf16[512,1536]{1,0:T(8,128)(2,1)}, bf16[512,1536]{1,0:T(8,128)(2,1)S(1)}, u32[]{:S(2)}, u32[]{:S(2)}) collective-permute-start(bf16[512,1536]{1,0:T(8,128)(2,1)} %fourier.16), channel_id=1, source_target_pairs={{0,2},{2,0},{1,3},{3,1},{4,6},{6,4},{5,7},{7,5},{8,10},{10,8},{9,1... | collective-permute-start | bytes 4718600 | tf_op jit(solution)/shard_map/ppermute | solution.py:393
  110.0 67.0 %all-to-all-start.1 = ((bf16[16,32,1536]{2,1,0:T(8,128)(2,1)}), bf16[16,32,1536]{2,1,0:T(8,128)(2,1)}, u32[]{:S(2)}, u32[]{:S(2)}) async-start(bf16[16,32,1536]{2,1,0:T(8,128)(2,1)} %bitcast.119), calls=%async_computation.1 | async-start | bytes 3145728 | tf_op jit(solution)/shard_map/all_to_all | solution.py:403
  123.6 45.5 %collective-permute-start.5 = (bf16[512,1920]{1,0:T(8,128)(2,1)}, bf16[512,1920]{1,0:T(8,128)(2,1)}, u32[]{:S(2)}, u32[]{:S(2)}) collective-permute-start(bf16[512,1920]{1,0:T(8,128)(2,1)} %fourier.18), channel_id=1, source_target_pairs={{0,2},{2,0},{1,3},{3,1},{4,6},{6,4},{5,7},{7,5},{8,10},{10,8},{9,1... | collective-permute-start | bytes 5898248 | tf_op jit(solution)/shard_map/ppermute | solution.py:393
  130.2 52.5 %collective-permute-start.6 = (bf16[12,160,640]{2,1,0:T(8,128)(2,1)}, bf16[12,160,640]{2,1,0:T(8,128)(2,1)S(1)}, u32[]{:S(2)}, u32[]{:S(2)}) collective-permute-start(bf16[12,160,640]{2,1,0:T(8,128)(2,1)} %get-tuple-element.43), channel_id=1, source_target_pairs={{0,1},{1,0},{2,3},{3,2},{4,5},{5,4},{6,7},{7,6},{8,9},{9,8},{10,11... | collective-permute-start | bytes 7372808 | tf_op jit(solution)/shard_map/ppermute | solution.py:389
  177.0 69.0 %all-to-all-start.2 = ((bf16[16,32,1920]{2,1,0:T(8,128)(2,1)}), bf16[16,32,1920]{2,1,0:T(8,128)(2,1)}, u32[]{:S(2)}, u32[]{:S(2)}) async-start(bf16[16,32,1920]{2,1,0:T(8,128)(2,1)} %bitcast.115), calls=%async_computation.2 | async-start | bytes 3932160 | tf_op jit(solution)/shard_map/all_to_all | solution.py:403
  191.6 45.3 %collective-permute-start.7 = (bf16[512,1920]{1,0:T(8,128)(2,1)}, bf16[512,1920]{1,0:T(8,128)(2,1)S(1)}, u32[]{:S(2)}, u32[]{:S(2)}) collective-permute-start(bf16[512,1920]{1,0:T(8,128)(2,1)} %fourier.20), channel_id=1, source_target_pairs={{0,2},{2,0},{1,3},{3,1},{4,6},{6,4},{5,7},{7,5},{8,10},{10,8},{9,1... | collective-permute-start | bytes 5898248 | tf_op jit(solution)/shard_map/ppermute | solution.py:393
  193.1 58.7 %collective-permute-start.8 = (bf16[12,160,640]{2,1,0:T(8,128)(2,1)}, bf16[12,160,640]{2,1,0:T(8,128)(2,1)S(1)}, u32[]{:S(2)}, u32[]{:S(2)}) collective-permute-start(bf16[12,160,640]{2,1,0:T(8,128)(2,1)} %get-tuple-element.42), channel_id=1, source_target_pairs={{0,1},{1,0},{2,3},{3,2},{4,5},{5,4},{6,7},{7,6},{8,9},{9,8},{10,11... | collective-permute-start | bytes 7372808 | tf_op jit(solution)/shard_map/ppermute | solution.py:389
  246.0 67.8 %all-to-all-start.3 = ((bf16[16,32,1920]{2,1,0:T(8,128)(2,1)}), bf16[16,32,1920]{2,1,0:T(8,128)(2,1)}, u32[]{:S(2)}, u32[]{:S(2)}) async-start(bf16[16,32,1920]{2,1,0:T(8,128)(2,1)} %bitcast.113), calls=%async_computation.3 | async-start | bytes 3932160 | tf_op jit(solution)/shard_map/all_to_all | solution.py:403
  260.6 45.4 %collective-permute-start.9 = (bf16[512,1920]{1,0:T(8,128)(2,1)}, bf16[512,1920]{1,0:T(8,128)(2,1)}, u32[]{:S(2)}, u32[]{:S(2)}) collective-permute-start(bf16[512,1920]{1,0:T(8,128)(2,1)} %fourier.22), channel_id=1, source_target_pairs={{0,2},{2,0},{1,3},{3,1},{4,6},{6,4},{5,7},{7,5},{8,10},{10,8},{9,1... | collective-permute-start | bytes 5898248 | tf_op jit(solution)/shard_map/ppermute | solution.py:393
  267.2 52.4 %collective-permute-start.10 = (bf16[12,160,640]{2,1,0:T(8,128)(2,1)}, bf16[12,160,640]{2,1,0:T(8,128)(2,1)S(1)}, u32[]{:S(2)}, u32[]{:S(2)}) collective-permute-start(bf16[12,160,640]{2,1,0:T(8,128)(2,1)} %get-tuple-element.41), channel_id=1, source_target_pairs={{0,1},{1,0},{2,3},{3,2},{4,5},{5,4},{6,7},{7,6},{8,9},{9,8},{10,11... | collective-permute-start | bytes 7372808 | tf_op jit(solution)/shard_map/ppermute | solution.py:389
  313.8 69.2 %all-to-all-start.4 = ((bf16[16,32,1920]{2,1,0:T(8,128)(2,1)}), bf16[16,32,1920]{2,1,0:T(8,128)(2,1)}, u32[]{:S(2)}, u32[]{:S(2)}) async-start(bf16[16,32,1920]{2,1,0:T(8,128)(2,1)} %bitcast.116), calls=%async_computation.4 | async-start | bytes 3932160 | tf_op jit(solution)/shard_map/all_to_all | solution.py:403
  328.6 45.3 %collective-permute-start.11 = (bf16[512,1920]{1,0:T(8,128)(2,1)}, bf16[512,1920]{1,0:T(8,128)(2,1)S(1)}, u32[]{:S(2)}, u32[]{:S(2)}) collective-permute-start(bf16[512,1920]{1,0:T(8,128)(2,1)} %fourier.24), channel_id=1, source_target_pairs={{0,2},{2,0},{1,3},{3,1},{4,6},{6,4},{5,7},{7,5},{8,10},{10,8},{9,1... | collective-permute-start | bytes 5898248 | tf_op jit(solution)/shard_map/ppermute | solution.py:393
  330.0 58.8 %collective-permute-start.12 = (bf16[12,160,640]{2,1,0:T(8,128)(2,1)}, bf16[12,160,640]{2,1,0:T(8,128)(2,1)S(1)}, u32[]{:S(2)}, u32[]{:S(2)}) collective-permute-start(bf16[12,160,640]{2,1,0:T(8,128)(2,1)} %get-tuple-element.40), channel_id=1, source_target_pairs={{0,1},{1,0},{2,3},{3,2},{4,5},{5,4},{6,7},{7,6},{8,9},{9,8},{10,11... | collective-permute-start | bytes 7372808 | tf_op jit(solution)/shard_map/ppermute | solution.py:389
  383.0 69.0 %all-to-all-start.5 = ((bf16[16,32,1920]{2,1,0:T(8,128)(2,1)}), bf16[16,32,1920]{2,1,0:T(8,128)(2,1)}, u32[]{:S(2)}, u32[]{:S(2)}) async-start(bf16[16,32,1920]{2,1,0:T(8,128)(2,1)} %bitcast.114), calls=%async_computation.5 | async-start | bytes 3932160 | tf_op jit(solution)/shard_map/all_to_all | solution.py:403
  397.7 45.3 %collective-permute-start.13 = (bf16[512,1920]{1,0:T(8,128)(2,1)}, bf16[512,1920]{1,0:T(8,128)(2,1)S(1)}, u32[]{:S(2)}, u32[]{:S(2)}) collective-permute-start(bf16[512,1920]{1,0:T(8,128)(2,1)} %fourier.26), channel_id=1, source_target_pairs={{0,2},{2,0},{1,3},{3,1},{4,6},{6,4},{5,7},{7,5},{8,10},{10,8},{9,1... | collective-permute-start | bytes 5898248 | tf_op jit(solution)/shard_map/ppermute | solution.py:393
  452.0 77.4 %all-to-all-start.6 = ((bf16[16,32,1920]{2,1,0:T(8,128)(2,1)}), bf16[16,32,1920]{2,1,0:T(8,128)(2,1)S(1)}, u32[]{:S(2)}, u32[]{:S(2)}) async-start(bf16[16,32,1920]{2,1,0:T(8,128)(2,1)} %bitcast.112), calls=%async_computation.6 | async-start | bytes 3932160 | tf_op jit(solution)/shard_map/all_to_all | solution.py:403
  557.6 3.9 collective-permute-start.15
  561.5 3.9 collective-permute-start.16
  569.2 4.8 collective-permute-start.18
  (24 other events, 63.9 us)
